TPU v7x, 32 devices: a whole 2x2x4 slice. The times are simulated.
32 devices in a mesh: row: 4 (over x, core), col: 8 (over z, y).
Axes of the slice: x: 2, y: 2, z: 4, core: 2. Of those that a mesh axis runs over, the one named last changes fastest.
Arguments:
- design: bfloat16 [18432, 2048], P(('row', 'col')), may hold values from -0.19921875 to 0.19921875
- arc_filter: bfloat16 [2048, 2048], replicated, may hold values from -0.59765625 to 0.59765625
- arc_of_row: int32 [2048], replicated, may hold values from 0 to 255, never falling along the last dimension, each value on 1 to 512 neighbouring positions
- terr_stored: bfloat16 [18432, 128], P(('row', 'col')), may hold values from -3 to 3
- block_order: int32 [144], P('row'), may hold values from 0 to 143, as said below
- directions: float32 [18432, 256], P(('row', 'col')), may hold values from -6 to 6
Outputs:
- normals: float32 [4, 8, 576, 18432], P(None, 'col', None, 'row')
- products: float32 [18432, 256], P(('row', 'col'))
Inputs may be any that keep to these rules, and one draw needn't show every extreme that they name: `arc_of_row`: arc numbers never fall along the observations. `block_order`: each aligned group of 36 consecutive entries (the blocks of one block of 4608 unknowns) is a permutation of the positions of that same group.
All inputs are finite; a program needn't handle non-finite values.
Results may differ from a plain program's by a relative error of at most 0.00045.
Values may be sent and summed in bfloat16 or wider, within the bound.
A program may use at most 192 MiB of HBM per device.

v0:
```python
import functools

import jax
import jax.numpy as jnp
import numpy as np
from jax import lax
from jax.experimental import pallas as pl
from jax.experimental.pallas import tpu as pltpu
from jax.sharding import PartitionSpec as P


HIGH = lax.Precision.HIGHEST
NT = (((1,), (1,)), ((), ()))
MESH = pl.DeviceIdType.MESH


def dot_high(a, b):
    return jnp.dot(a, b, precision=HIGH, preferred_element_type=jnp.float32)


def whiten(design, arc_filter, arc_of_row):
    positions = jnp.arange(arc_filter.shape[0], dtype=jnp.int32)
    keep_mask = (positions[:, None] > positions[None, :]) & (
        arc_of_row[:, None] == arc_of_row[None, :]
    )
    lower_part = jnp.where(keep_mask, arc_filter, jnp.zeros_like(arc_filter))
    mixed_part = lax.dot_general(design, lower_part, NT, preferred_element_type=jnp.float32)
    return (design.astype(jnp.float32) + mixed_part).astype(jnp.bfloat16)


def general_body(design, arc_filter, arc_of_row, terr_stored, block_order, directions):
    whitened = whiten(design, arc_filter, arc_of_row)
    own_width = whitened.shape[0]
    rows_block, terr_rows = (
        lax.all_gather(whitened, "col", axis=0, tiled=True),
        lax.all_gather(terr_stored, "col", axis=0, tiled=True),
    )
    cols_block = lax.all_gather(whitened, "row", axis=0, tiled=True)
    normal_tile = lax.dot_general(cols_block, rows_block, NT, preferred_element_type=jnp.float32)
    block_size = terr_rows.shape[1]
    span_rows = terr_rows.shape[0]
    group_count = span_rows // block_size
    row_index = lax.axis_index("row")
    col_index = lax.axis_index("col")
    local_order = block_order - row_index * group_count
    selector = (local_order[None, :] == jnp.arange(group_count, dtype=jnp.int32)[:, None]).astype(
        jnp.float32
    )
    stored = terr_rows.astype(jnp.float32).reshape(group_count, block_size, block_size)
    symmetric = jnp.triu(stored) + jnp.swapaxes(jnp.triu(stored, 1), 1, 2)
    ordered = jnp.einsum("qt,tab->qab", selector, symmetric, precision=HIGH).reshape(
        span_rows, block_size
    )
    own_rows = lax.dynamic_slice_in_dim(ordered, col_index * own_width, own_width, 0)
    positions = col_index * own_width + jnp.arange(own_width, dtype=jnp.int32)
    onehot = (
        (positions // block_size)[:, None] == jnp.arange(group_count, dtype=jnp.int32)[None, :]
    ).astype(jnp.float32)
    terr_added = (onehot[:, :, None] * own_rows[:, None, :]).reshape(own_width, span_rows)
    current = lax.dynamic_slice_in_dim(normal_tile, row_index * own_width, own_width, 0)
    normal_tile = lax.dynamic_update_slice_in_dim(
        normal_tile, current + terr_added, row_index * own_width, 0
    )
    tile_rows = normal_tile.shape[0]
    partial_sum = dot_high(normal_tile, lax.all_gather(directions, "col", axis=0, tiled=True))
    products = lax.psum_scatter(partial_sum, "row", scatter_dimension=0, tiled=True)
    normals = normal_tile.reshape(tile_rows // own_width, 1, own_width, span_rows)
    return (normals, products)


def xor(i, mask):
    return i + mask * (1 - 2 * ((i // mask) % 2))


def split3(x):
    a = x.astype(jnp.bfloat16)
    rest = x - a.astype(jnp.float32)
    b = rest.astype(jnp.bfloat16)
    return a, b, (rest - b.astype(jnp.float32)).astype(jnp.bfloat16)


def wide3(x):
    return jnp.concatenate(split3(x), 1)


def fold3(x):
    n = x.shape[1] // 3
    return x[:, 2 * n :] + x[:, n : 2 * n] + x[:, :n]


def whiten_kernel(d_ref, dp_ref, f_ref, fp_ref, ac_ref, ar_ref, arp_ref, dir_ref, w_ref, v_ref):
    b = pl.program_id(0)
    width = f_ref.shape[0]
    zero = jnp.zeros((width, width), jnp.float32)
    k = lax.broadcasted_iota(jnp.int32, (width, width), 0)
    j = lax.broadcasted_iota(jnp.int32, (width, width), 1)
    keep = (k > j) & (ac_ref[...] == ar_ref[...])
    keep_prev = (ac_ref[...] == arp_ref[...]) & (b > 0)
    here = jnp.where(keep, f_ref[...].astype(jnp.float32), zero).astype(jnp.bfloat16)
    prev = jnp.where(keep_prev, fp_ref[...].astype(jnp.float32), zero).astype(jnp.bfloat16)
    mixed = lax.dot_general(d_ref[...], here, NT, preferred_element_type=jnp.float32)
    mixed += lax.dot_general(dp_ref[...], prev, NT, preferred_element_type=jnp.float32)
    out = (d_ref[...].astype(jnp.float32) + mixed).astype(jnp.bfloat16)
    w_ref[...] = out
    v_ref[...] = fold3(
        lax.dot_general(
            out,
            wide3(dir_ref[...]),
            (((0,), (0,)), ((), ())),
            preferred_element_type=jnp.float32,
        )
    )


def whiten_rows(design, arc_filter, arc_of_row, directions):
    own, total = design.shape
    width = total // 4
    cols = directions.shape[1]
    here = lambda b: (0, b)
    prev = lambda b: (0, jnp.maximum(b - 1, 0))
    row = arc_of_row.reshape(1, total)
    return pl.pallas_call(
        whiten_kernel,
        grid=(total // width,),
        in_specs=[
            pl.BlockSpec((own, width), here),
            pl.BlockSpec((own, width), prev),
            pl.BlockSpec((width, width), lambda b: (b, b)),
            pl.BlockSpec((width, width), lambda b: (b, jnp.maximum(b - 1, 0))),
            pl.BlockSpec((width, 1), lambda b: (b, 0)),
            pl.BlockSpec((1, width), here),
            pl.BlockSpec((1, width), prev),
            pl.BlockSpec((own, cols), lambda b: (0, 0)),
        ],
        out_specs=[
            pl.BlockSpec((own, width), here),
            pl.BlockSpec((width, cols), lambda b: (b, 0)),
        ],
        out_shape=[
            jax.ShapeDtypeStruct((own, total), jnp.bfloat16),
            jax.ShapeDtypeStruct((total, cols), jnp.float32),
        ],
        name="whiten",
        cost_estimate=pl.CostEstimate(
            flops=4 * own * total * width, bytes_accessed=8 * own * total, transcendentals=0
        ),
    )(design, design, arc_filter, arc_filter, arc_of_row.reshape(total, 1), row, row, directions)


def masks_of(n):
    return [1 << i for i in range(n.bit_length() - 1)]


def exchange_kernel(n_row, n_col, parts, w_ref, t_ref, d_ref, v_ref, *refs):
    rows_ref, up1, up2a, up2b, dn1, dn2a, dn2b, terr_ref, edge_ref, vout = refs[:10]
    stage, got, acc, s_loc, s_ring, r_ring, s_row, r_row, s_terr, r_terr, s_v, r_v, s_e, r_e = refs[10:]
    r = lax.axis_index("row")
    c = lax.axis_index("col")
    own = w_ref.shape[0]
    sub = own // parts
    zs = n_col // 2
    z, y = c // 2, c % 2
    place = z + y * (n_col - 1 - 2 * z)

    def col_at(p):
        side = p // zs
        return 2 * (p + side * (n_col - 1 - 2 * p)) + side

    nxt = col_at((place + 1) % n_col)
    prv = col_at((place + n_col - 1) % n_col)
    row_masks, col_masks = masks_of(n_row), masks_of(n_col)
    peers = [(r, nxt), (r, prv)]
    peers += [(xor(r, m), c) for m in row_masks] + [(r, xor(c, m)) for m in col_masks]
    barrier = pltpu.get_barrier_semaphore()
    for peer in peers:
        pl.semaphore_signal(barrier, inc=1, device_id=peer, device_id_type=MESH)
    pl.semaphore_wait(barrier, len(peers))

    def remote(src, dst, ssem, rsem, peer):
        return pltpu.make_async_remote_copy(
            src_ref=src, dst_ref=dst, send_sem=ssem, recv_sem=rsem, device_id=peer,
            device_id_type=MESH,
        )

    def piece(ref, j):
        return ref.at[pl.ds(j * sub, sub)]

    steps = 2 * parts
    half = parts // 2

    def ring(s, way):
        one, two = ((up1, (up2a, up2b)), (dn1, (dn2a, dn2b)))[way]
        j = s % parts
        if s < parts:
            src, dst = piece(w_ref, j), piece(one, j)
        else:
            src, dst = piece(one, j), piece(two[j // half], j % half)
        return remote(src, dst, s_ring.at[way, s], r_ring.at[way, s], (r, (nxt, prv)[way]))

    rings = [[ring(s, way) for way in range(2)] for s in range(steps)]

    sends = []

    def start(copy):
        copy.start()
        sends.append(copy)

    far = n_col // 2

    def terr(k, way):
        src = t_ref if k == 1 else terr_ref.at[(n_col - k + 1) if way == 0 else k - 1]
        at = (n_col - k) if way == 0 else k
        return remote(src, terr_ref.at[at], s_terr.at[way, k - 1], r_terr.at[way, k - 1],
                      (r, (nxt, prv)[way]))

    terrs = {}
    for k in range(1, far + 1):
        terrs[k] = [terr(k, 0)] + ([terr(k, 1)] if k < far else [])

    total = v_ref.shape[0]
    levels = [("row", m) for m in row_masks] + [("col", m) for m in col_masks]
    span = total
    offset = 0
    gives, keeps, backs, spots = [], [], [], []
    base = 0
    for i, (axis, m) in enumerate(levels):
        at = r if axis == "row" else c
        peer = (xor(r, m), c) if axis == "row" else (r, xor(c, m))
        bit = (at // m) % 2
        span //= 2
        give = pl.ds(pl.multiple_of(offset + (1 - bit) * span, span), span)
        offset = offset + bit * span
        keep = pl.ds(pl.multiple_of(offset, span), span)
        src = (v_ref if i == 0 else acc).at[give]
        spot = pl.ds(base, span)
        base += span
        gives.append(remote(src, got.at[spot], s_v.at[i], r_v.at[i], peer))
        n = len(levels)
        backs.append(remote(vout.at[keep], vout.at[keep], s_v.at[n + i], r_v.at[n + i], peer))
        keeps.append(keep)
        spots.append(spot)

    def add(i):
        gives[i].wait()
        held = v_ref if i == 0 else acc
        into = vout if i == len(levels) - 1 else acc
        into[keeps[i]] = held[keeps[i]] + got[spots[i]]

    chain = []
    for i in range(len(levels)):
        chain.append(("give", i))
    for i in reversed(range(len(levels))):
        chain.append(("back", i))

    state = [0]

    def v_next():
        at = state[0]
        if at > len(chain):
            return
        if at > 0:
            kind, i = chain[at - 1]
            if kind == "give":
                add(i)
            else:
                backs[i].wait()
        if at < len(chain):
            kind, i = chain[at]
            (gives if kind == "give" else backs)[i].start()
        state[0] = at + 1

    def row_copy(m, mask, j):
        src = w_ref if m == mask else rows_ref.at[m - mask]
        n = row_index[(m, mask)]
        return remote(piece(src, j), piece(rows_ref.at[m], j), s_row.at[n, j], r_row.at[n, j],
                      (xor(r, mask), c))

    row_index = {}
    order = []
    for mask in reversed(row_masks):
        for m in range(0, n_row, 2 * mask):
            row_index[(m + mask, mask)] = len(row_index)
            order.append((m + mask, mask))

    v_next()
    for copy in terrs[1]:
        start(copy)
    for s in range(2):
        for way in range(2):
            start(rings[s][way])
    mine = pltpu.make_async_copy(w_ref, stage, s_loc.at[0])
    mine.start()
    edge = edge_ref.shape[0]
    edge_at = pl.ds(pl.multiple_of((1 - y) * (own - edge), 8), edge)
    edges = remote(d_ref.at[edge_at], edge_ref, s_e, r_e, (r, xor(c, 1)))
    start(edges)
    v_next()
    copies = {key: [row_copy(*key, j) for j in range(parts)] for key in order}
    first = [key for key in order if key[0] == key[1]]
    later = [key for key in order if key[0] != key[1]]
    for key in first:
        for copy in copies[key]:
            start(copy)
    mine.wait()
    put = pltpu.make_async_copy(stage, rows_ref.at[0], s_loc.at[1])
    put.start()

    hop = 1
    waited = set()
    for s in range(steps):
        for way in range(2):
            rings[s][way].wait_recv()
        if s % 2 == 0 or s > steps - 4:
            v_next()
        if s % 2 == 1 and hop <= far:
            for copy in terrs[hop]:
                copy.wait_recv()
            hop += 1
            if hop <= far:
                for copy in terrs[hop]:
                    start(copy)
        if s + 2 < steps:
            for way in range(2):
                start(rings[s + 2][way])
        j = s - 2
        if 0 <= j < parts:
            for key in later:
                m, mask = key
                up = [k for k in order if k[0] == m - mask][0]
                if (up, j) not in waited:
                    copies[up][j].wait_recv()
                    waited.add((up, j))
                start(copies[key][j])
    while hop <= far:
        for copy in terrs[hop]:
            copy.wait_recv()
        hop += 1
        if hop <= far:
            for copy in terrs[hop]:
                start(copy)
    while state[0] <= len(chain):
        v_next()
    for key in order:
        for j in range(parts):
            if (key, j) not in waited:
                copies[key][j].wait_recv()
    edges.wait_recv()
    put.wait()
    for copy in sends:
        copy.wait_send()


def exchange(n_row, n_col, whitened, terr_stored, directions, partial):
    own, total = whitened.shape
    cols = directions.shape[1]
    block = terr_stored.shape[1]
    parts = 6
    far = n_col // 2
    any_spec = pl.BlockSpec(memory_space=pl.ANY)
    vmem = pl.BlockSpec(memory_space=pltpu.VMEM)
    whole = jax.ShapeDtypeStruct((own, total), jnp.bfloat16)
    part = jax.ShapeDtypeStruct((own // 2, total), jnp.bfloat16)
    levels = n_row.bit_length() + n_col.bit_length() - 2
    moves = n_row - 1
    dma = pltpu.SemaphoreType.DMA
    return pl.pallas_call(
        functools.partial(exchange_kernel, n_row, n_col, parts),
        in_specs=[any_spec, any_spec, any_spec, vmem],
        out_specs=[any_spec] * 9 + [vmem],
        out_shape=[
            jax.ShapeDtypeStruct((n_row, own, total), jnp.bfloat16),
            whole, part, part, whole, part, part,
            jax.ShapeDtypeStruct((n_col, own, block), jnp.bfloat16),
            jax.ShapeDtypeStruct((block // 2, cols), jnp.float32),
            jax.ShapeDtypeStruct((total, cols), jnp.float32),
        ],
        scratch_shapes=[
            pltpu.VMEM((own, total), jnp.bfloat16),
            pltpu.VMEM((total, cols), jnp.float32),
            pltpu.VMEM((total, cols), jnp.float32),
            dma((2,)),
            dma((2, 2 * parts)), dma((2, 2 * parts)),
            dma((moves, parts)), dma((moves, parts)),
            dma((2, far)), dma((2, far)),
            dma((2 * levels,)), dma((2 * levels,)),
            dma(()), dma(()),
        ],
        name="exchange",
        compiler_params=pltpu.CompilerParams(
            collective_id=0, has_side_effects=True, vmem_limit_bytes=56 * 1024 * 1024
        ),
        cost_estimate=pl.CostEstimate(
            flops=1000000, bytes_accessed=40 * own * total, transcendentals=0
        ),
    )(whitened, terr_stored, directions, partial)


def products_kernel(order_ref, spot_ref, s_ref, t0_ref, t_ref, w_ref, v_ref, d_ref, e_ref,
                    p_ref, o_ref, inv_ref):
    own, span = o_ref.shape
    half = e_ref.shape[0]
    block = 2 * half
    per = own // half
    count = order_ref.shape[0]

    @pl.loop(0, count)
    def _(t):
        inv_ref[order_ref[t]] = t

    side = s_ref[1]
    o_ref[...] = jnp.zeros(o_ref.shape, o_ref.dtype)
    p_ref[...] = fold3(
        jnp.dot(w_ref[...], wide3(v_ref[...]), preferred_element_type=jnp.float32)
    )
    k = lax.broadcasted_iota(jnp.int32, (block, block), 0)
    j = lax.broadcasted_iota(jnp.int32, (block, block), 1)

    def stored(g):
        slot, at = spot_ref[g // per], g % per
        there = pl.ds(pl.multiple_of(at * half, half), half)
        return jnp.where(
            slot == 0,
            t0_ref[there, :].astype(jnp.float32),
            t_ref[slot, there, :].astype(jnp.float32),
        )

    edge = e_ref[...]
    for q in range(span // block):
        lo = 2 * q

        @pl.when((lo + 1 >= side * per) & (lo < side * per + per))
        def _(q=q, lo=lo):
            t = inv_ref[s_ref[0] + q]
            s = jnp.concatenate([stored(2 * t), stored(2 * t + 1)], 0)
            sym = jnp.where(k <= j, s, 0.0) + jnp.where(k < j, s, 0.0).T
            for h in range(2):
                i = lo + h - side * per

                @pl.when((i >= 0) & (i < per))
                def _():
                    mine = pl.ds(pl.multiple_of(i * half, half), half)
                    o_ref[mine, q * block : (q + 1) * block] = sym[h * half : (h + 1) * half]
                    other = i + 1 - 2 * h
                    inside = (other >= 0) & (other < per)
                    safe = jnp.minimum(jnp.maximum(other, 0), per - 1)
                    pair = d_ref[pl.ds(pl.multiple_of(safe * half, half), half), :]
                    pair = jnp.where(inside, pair, edge)
                    this = d_ref[mine, :]
                    near = jnp.concatenate([pair, this] if h else [this, pair], 0)
                    rows = sym[h * half : (h + 1) * half].astype(jnp.bfloat16)
                    p_ref[mine, :] += fold3(
                        jnp.dot(rows, wide3(near), preferred_element_type=jnp.float32)
                    )


def products_job(order, spots, scalars, terr_stored, terr_all, whitened, v, directions, edge):
    own = whitened.shape[0]
    cols = directions.shape[1]
    vmem = pl.BlockSpec(memory_space=pltpu.VMEM)
    smem = pl.BlockSpec(memory_space=pltpu.SMEM)
    return pl.pallas_call(
        products_kernel,
        in_specs=[smem] * 3 + [vmem] * 6,
        out_specs=[vmem] * 2,
        out_shape=[
            jax.ShapeDtypeStruct((own, cols), jnp.float32),
            jax.ShapeDtypeStruct((own, 2 * own), jnp.float32),
        ],
        scratch_shapes=[pltpu.SMEM((order.shape[0],), jnp.int32)],
        name="products",
        compiler_params=pltpu.CompilerParams(vmem_limit_bytes=40 * 1024 * 1024),
        cost_estimate=pl.CostEstimate(
            flops=6 * own * whitened.shape[1] * cols, bytes_accessed=10000000, transcendentals=0
        ),
    )(order, spots, scalars, terr_stored, terr_all, whitened, v, directions, edge)


def tile_kernel(wants, sources, width, first, terr, s_ref, *refs):
    n = 1 + max(at for pair in sources.values() for at, _ in pair)
    bufs = refs[:n]
    a_ref = refs[n]
    rest = refs[n + 1 :]
    if terr:
        t_ref, rest = rest[0], rest[1:]
    o_hbm, b_ref, o_ref, sem, o_sem = rest if first else rest[1:]
    i = pl.program_id(0)
    steps = pl.num_programs(0)
    own = a_ref.shape[1]
    half = own // 2
    span = b_ref.shape[0]
    lo = s_ref[4]

    def copy(k, y, h):
        at, row = sources[k][h]
        return pltpu.make_async_copy(
            bufs[at].at[pl.ds(row, half)],
            b_ref.at[pl.ds((2 * y + h) * half, half)],
            sem.at[2 * y + h],
        )

    @pl.when(i == 0)
    def _():
        for y in range(2):
            for h in range(2):
                needed = wants(s_ref, y, h)
                for k in sources:

                    @pl.when((s_ref[1 + y] == k) & needed)
                    def _():
                        copy(k, y, h).start()

        for y in range(2):
            for h in range(2):

                @pl.when(wants(s_ref, y, h))
                def _():
                    copy(next(iter(sources)), y, h).wait()

    slot = i % 2

    def out(i, slot):
        return pltpu.make_async_copy(
            o_ref.at[slot],
            o_hbm.at[
                pl.ds(pl.multiple_of(s_ref[6 + i] * own, own), own),
                pl.ds(pl.multiple_of(s_ref[0] * span + lo, 128), width),
            ],
            o_sem.at[slot],
        )

    @pl.when(i >= 2)
    def _():
        out(i - 2, slot).wait()

    o_ref[slot] = lax.dot_general(
        a_ref[0],
        b_ref[pl.ds(pl.multiple_of(lo, 128), width), :],
        NT,
        preferred_element_type=jnp.float32,
    )
    if terr:

        @pl.when((i == 0) & (s_ref[3] == 1))
        def _():
            o_ref[slot] += t_ref[...]

    out(i, slot).start()

    @pl.when(i == steps - 1)
    def _():
        out(i - 1, 1 - slot).wait()
        out(i, slot).wait()


def tile_job(scalars, wants, cands, bufs, rows, width, terr, out):
    count, own, total = rows.shape
    span = 2 * own
    first = not isinstance(out, jax.Array)
    any_spec = pl.BlockSpec(memory_space=pl.ANY)
    arrays, sources = [], {}
    for k in cands:
        pair = []
        for array, row in bufs[k]:
            at = [i for i, a in enumerate(arrays) if a is array]
            if not at:
                arrays.append(array)
                at = [len(arrays) - 1]
            pair.append((at[0], row))
        sources[k] = pair
    operands = arrays + [rows]
    in_specs = [any_spec] * len(arrays) + [
        pl.BlockSpec((1, own, total), lambda i, s: (i, 0, 0)),
    ]
    if terr is not None:
        operands.append(terr)
        in_specs.append(pl.BlockSpec((own, span), lambda i, s: (0, 0)))
    shape = out
    alias = {}
    if not first:
        alias = {1 + len(operands): 0}
        operands.append(out)
        in_specs.append(any_spec)
        shape = jax.ShapeDtypeStruct(out.shape, out.dtype)
    return pl.pallas_call(
        functools.partial(tile_kernel, wants, sources, width, first, terr is not None),
        grid_spec=pltpu.PrefetchScalarGridSpec(
            num_scalar_prefetch=1,
            grid=(count,),
            in_specs=in_specs,
            out_specs=any_spec,
            scratch_shapes=[
                pltpu.VMEM((span, total), jnp.bfloat16),
                pltpu.VMEM((2, own, width), jnp.float32),
                pltpu.SemaphoreType.DMA((4,)),
                pltpu.SemaphoreType.DMA((2,)),
            ],
        ),
        out_shape=shape,
        input_output_aliases=alias,
        compiler_params=pltpu.CompilerParams(vmem_limit_bytes=48 * 1024 * 1024),
        cost_estimate=pl.CostEstimate(
            flops=2 * count * own * width * total,
            bytes_accessed=2 * count * own * total + 4 * count * own * width,
            transcendentals=0,
        ),
    )(scalars, *operands)


def ring_body(n_row, n_col, design, arc_filter, arc_of_row, terr_stored, block_order, directions):
    own, _ = design.shape
    block = terr_stored.shape[1]
    r = lax.axis_index("row")
    c = lax.axis_index("col")
    zs = n_col // 2
    half = own // 2
    far = n_col // 2

    def hop(a, perm):
        return lax.ppermute(a, "col", perm)

    col_of = [2 * p if p < zs else 2 * (n_col - 1 - p) + 1 for p in range(n_col)]
    pos_of = [0] * n_col
    for p, col in enumerate(col_of):
        pos_of[col] = p
    forward = [(col_of[p], col_of[(p + 1) % n_col]) for p in range(n_col)]
    backward = [(d, s) for s, d in forward]

    whitened, partial = whiten_rows(design, arc_filter, arc_of_row, directions)
    rows, up1, up2a, up2b, dn1, dn2a, dn2b, terr_all, edge, v = exchange(
        n_row, n_col, whitened, terr_stored, directions, partial
    )
    bufs = {
        0: [(whitened, 0), (whitened, half)],
        1: [(dn1, 0), (dn1, half)],
        2: [(dn2a, 0), (dn2b, 0)],
        n_col - 1: [(up1, 0), (up1, half)],
        n_col - 2: [(up2a, 0), (up2b, 0)],
    }
    for k in range(3, far + 1):
        before_up, before_dn = bufs[n_col - k + 1], bufs[k - 1]
        if k < far:
            ua = hop(before_up[0][0], forward)
            db = hop(before_dn[1][0], backward)
            ub = hop(before_up[1][0], forward)
            da = hop(before_dn[0][0], backward)
            bufs[n_col - k] = [(ua, 0), (ub, 0)]
            bufs[k] = [(da, 0), (db, 0)]
        else:
            ua = hop(before_up[0][0], forward)
            db = hop(before_dn[1][0], backward)
            bufs[k] = [(ua, 0), (db, 0)]

    per_pair = 2 * own // block
    count = per_pair * zs
    spots = np.array([[(pos_of[d] - pos_of[s]) % n_col for d in range(n_col)] for s in range(n_col)])
    local_order = block_order - r * count
    products, terr = products_job(
        local_order,
        jnp.asarray(spots, jnp.int32)[c],
        jnp.stack([(c // 2) * per_pair, c % 2]).astype(jnp.int32),
        terr_stored, terr_all, whitened, v, directions, edge,
    )

    wide = own // 128 * 128
    table = np.zeros((zs, n_col, 6), np.int32)
    for col in range(n_col):
        jobs = []
        for zz in range(zs):
            ks = [(pos_of[2 * zz + yy] - pos_of[col]) % n_col for yy in range(2)]
            ready = max(min(k, n_col - k) for k in ks)
            jobs.append((ready, zz, ks))
        for j, (_, zz, ks) in enumerate(sorted(jobs)):
            late = ks.index(far) if far in ks else 0
            table[j, col] = [zz, ks[0], ks[1], int(zz == col // 2), 0, late]
    row_spots = jnp.bitwise_xor(r, jnp.arange(n_row, dtype=jnp.int32))
    out = jax.ShapeDtypeStruct((n_row * own, n_col * own), jnp.float32)

    def job(j, wants, cands, width, terr, out, spot=None):
        use = table[j].copy()
        if spot is not None:
            use[:, 4] = [spot(late) for late in use[:, 5]]
        scalars = jnp.concatenate([jnp.asarray(use)[c], row_spots])
        return tile_job(scalars, wants, cands, bufs, rows, width, terr, out)

    every = lambda s, y, h: s[5] >= 0
    early = lambda s, y, h: s[5] == 1 - y
    tail = lambda s, y, h: (s[5] == y) | (h == 1 - y)
    for j in range(zs - 1):
        cands = tuple(sorted(set(table[j, :, 1:3].ravel().tolist())))
        out = job(j, every, cands, 2 * own, terr, out)
    cands = set(table[zs - 1, :, 1:3].ravel().tolist())
    out = job(zs - 1, early, tuple(sorted(cands - {far})), wide, None, out,
              lambda late: 0 if late == 1 else 2 * own - wide)
    out = job(zs - 1, tail, tuple(sorted(cands)), 2 * own - wide, None, out,
              lambda late: wide if late == 1 else 0)
    return out.reshape(n_row, 1, own, n_col * own), products


def power_of_two(n):
    return n > 1 and n & (n - 1) == 0


def solution(mesh):
    n_row, n_col = mesh.shape["row"], mesh.shape["col"]

    def body(design, arc_filter, arc_of_row, terr_stored, block_order, directions):
        args = (design, arc_filter, arc_of_row, terr_stored, block_order, directions)
        own, block = design.shape[0], terr_stored.shape[1]
        aligned = own % 192 == 0 and own % block == block // 2 and (2 * own) % 128 == 0
        if power_of_two(n_row) and power_of_two(n_col) and n_col > 6 and aligned:
            return ring_body(n_row, n_col, *args)
        return general_body(*args)

    return jax.shard_map(
        body,
        mesh=mesh,
        in_specs=(
            P(("row", "col"), None),
            P(),
            P(),
            P(("row", "col"), None),
            P("row"),
            P(("row", "col"), None),
        ),
        out_specs=(P(None, "col", None, "row"), P(("row", "col"), None)),
        check_vma=False,
    )
```

profile of v0, /device:TPU:0, one launch (start us, length us, event | category | flops | bytes accessed | tf_op | source)
XLA Modules:
  0.0 278.6 jit_solution(8996026816888359252)
XLA Ops:
  0.6 2.1 copy.19.ac_ref
  2.7 13.8 %whiten.1 = (bf16[576,2048]{1,0:T(8,128)(2,1)}, f32[2048,256]{1,0:T(8,128)}) custom-call(bf16[576,2048]{1,0:T(8,128)(2,1)} %dp_ref.1, bf16[576,2048]{1,0:T(8,128)(2,1)} %dp_ref.1, bf16[2048,2048]{1,0:T(8,128)(2,1)} %fp_ref.1, bf16[2048,2048]{1,0:T(8,128)(2,1)} %fp_ref.1, s32[2048,1]{1,0:T(8,128)} %copy.19.ac_ref, s32[1,2048]{1,0:T(1,128)} %bitcast.21, ...), custom_call_target="tpu_custom_call" | custom-call | flops 2415919104 | bytes 9437184 | tf_op jit(solution)/shard_map/whiten/pallas_call | solution.py:122
  16.5 143.5 %exchange.1 = (bf16[4,576,2048]{2,1,0:T(8,128)(2,1)}, bf16[576,2048]{1,0:T(8,128)(2,1)}, bf16[288,2048]{1,0:T(8,128)(2,1)}, bf16[288,2048]{1,0:T(8,128)(2,1)}, b...) custom-call(bf16[576,2048]{1,0:T(8,128)(2,1)} %get-tuple-element.16., ...), custom_call_target="tpu_custom_call" | custom-call | flops 1000000 | bytes 47185920 | tf_op jit(solution)/shard_map/exchange/pallas_call | solution.py:366
  160.0 0.1 collective-permute-start.1
  160.1 2.0 collective-permute-start.2
  162.1 0.1 collective-permute-start
  162.2 2.0 collective-permute-start.5
  164.1 0.7 fusion.3.spot_ref
  164.8 0.7 fusion
  165.5 0.1 pad_add_fusion.3.s_ref
  165.6 0.7 fusion.1
  166.3 0.7 fusion.4
  167.0 0.1 pad_add_fusion.s_ref
  167.1 0.1 pad_add_fusion.5
  167.2 1.1 copy-done.6
  168.2 0.9 copy-done.7
  169.1 1.6 copy-done.8
  170.7 1.3 copy-done.9
  172.0 0.8 copy-done.10
  172.9 6.1 %products.1 = (f32[576,256]{1,0:T(8,128)}, f32[576,1152]{1,0:T(8,128)S(1)}) custom-call(s32[36]{0:T(128)S(1)} %broadcast_subtract_fusion.order_ref, s32[8]{0:T(128)S(1)} %fusion.3.spot_ref, s32[2]{0:T(128)S(1)} %pad_add_fusion.3.s_ref, bf16[576,128]{1,0:T(8,128)(2,1)S(1)} %copy-done.7, bf16[8,576,128]{2,1,0:T(8,128)(2,1)S(1)} %copy-done.9, ...), custom_call_target="tpu_custom_call" | custom-call | flops 1811939328 | bytes 10000000 | tf_op jit(solution)/shard_map/products/pallas_call | solution.py:461
  179.0 1.6 copy-done.1
  180.6 20.4 %shard_map.131.refs_13_ = f32[2304,4608]{1,0:T(8,128)} custom-call(s32[10]{0:T(128)S(1)} %get-tuple-element.34.s_ref, bf16[576,2048]{1,0:T(8,128)(2,1)} %get-tuple-element.16.w_ref.refs_0_, bf16[576,2048]{1,0:T(8,128)(2,1)} %get-tuple-element.18.refs_1_.refs_0_, bf16[288,2048]{1,0:T(8,128)(2,1)S(1)} %copy-done.4, bf16[288,2048]{1,0:T(8,128)(2,1)S(1)} %copy-done.5, ...), custom_call_target="tpu_custom_call" | custom-call | flops 10871635968 | bytes 20054016 | tf_op jit(solution)/shard_map/pallas_call | solution.py:584
  201.0 0.0 collective-permute-done.2.refs_6_.refs_5_.refs_3_
  201.0 0.1 collective-permute-start.3
  201.1 2.0 collective-permute-start.4
  203.1 11.4 %collective-permute-done.refs_4_.refs_3_.refs_1_ = bf16[288,2048]{1,0:T(8,128)(2,1)} collective-permute-done((bf16[288,2048]{1,0:T(8,128)(2,1)}, bf16[288,2048]{1,0:T(8,128)(2,1)}, u32[]{:S(2)}, u32[]{:S(2)}) %collective-permute-start) | collective-permute-done | bytes 1179680 | tf_op jit(solution)/shard_map/ppermute | solution.py:619
  214.5 0.1 collective-permute-done.5.refs_7_.refs_6_.refs_4_
  214.6 20.2 %shard_map.132.refs_11_ = f32[2304,4608]{1,0:T(8,128)} custom-call(s32[10]{0:T(128)S(1)} %get-tuple-element.37.s_ref, bf16[576,2048]{1,0:T(8,128)(2,1)} %get-tuple-element.16.w_ref.refs_0_, bf16[576,2048]{1,0:T(8,128)(2,1)} %get-tuple-element.18.refs_1_.refs_0_, bf16[288,2048]{1,0:T(8,128)(2,1)S(1)} %copy-done.4, ...), custom_call_target="tpu_custom_call", output_to_operand_aliasing={{}: (14, {})} | custom-call | flops 10871635968 | bytes 20054016 | tf_op jit(solution)/shard_map/pallas_call | solution.py:584
  234.8 19.9 %shard_map.133.refs_7_ = f32[2304,4608]{1,0:T(8,128)} custom-call(s32[10]{0:T(128)S(1)} %get-tuple-element.36.s_ref, bf16[576,2048]{1,0:T(8,128)(2,1)} %get-tuple-element.16.w_ref.refs_0_, bf16[288,2048]{1,0:T(8,128)(2,1)S(1)} %copy-done.4, bf16[288,2048]{1,0:T(8,128)(2,1)S(1)} %copy-done.5, ...), custom_call_target="tpu_custom_call", output_to_operand_aliasing={{}: (12, {})} | custom-call | flops 10871635968 | bytes 20054016 | tf_op jit(solution)/shard_map/pallas_call | solution.py:584
  254.7 11.3 %shard_map.134.refs_9_ = f32[2304,4608]{1,0:T(8,128)} custom-call(s32[10]{0:T(128)S(1)} %get-tuple-element.35.s_ref, bf16[576,2048]{1,0:T(8,128)(2,1)} %get-tuple-element.18.refs_1_.refs_0_, bf16[288,2048]{1,0:T(8,128)(2,1)} %collective-permute-done.refs_4_.refs_3_.refs_1_, ...), custom_call_target="tpu_custom_call", output_to_operand_aliasing={{}: (8, {})} | custom-call | flops 4831838208 | bytes 14155776 | tf_op jit(solution)/shard_map/pallas_call | solution.py:584
  266.0 0.0 collective-permute-done.4.refs_4_
  266.0 12.5 %shard_map.135 = f32[2304,4608]{1,0:T(8,128)} custom-call(s32[10]{0:T(128)S(1)} %pad_add_fusion.s_ref, bf16[576,2048]{1,0:T(8,128)(2,1)} %get-tuple-element.18.refs_1_.refs_0_, bf16[288,2048]{1,0:T(8,128)(2,1)} %collective-permute-done.refs_4_.refs_3_.refs_1_, ...), custom_call_target="tpu_custom_call", output_to_operand_aliasing={{}: (10, {})} | custom-call | flops 6039797760 | bytes 15335424 | tf_op jit(solution)/shard_map/pallas_call | solution.py:584
  (22 shorter events, 0.0 us)
Async XLA Ops:
  16.5 149.1 %copy-start.11 = (s32[36]{0:T(128)S(1)}, s32[36]{0:T(128)}, u32[]{:S(2)}) copy-start(s32[36]{0:T(128)} %param.16) | copy-start | bytes 436
  16.5 150.6 %copy-start = (bf16[576,2048]{1,0:T(8,128)(2,1)S(1)}, bf16[576,2048]{1,0:T(8,128)(2,1)}, u32[]{:S(2)}) copy-start(bf16[576,2048]{1,0:T(8,128)(2,1)} %get-tuple-element.16.w_ref.refs_0_) | copy-start | bytes 7077892
  160.0 41.0 %collective-permute-start.1 = (bf16[288,2048]{1,0:T(8,128)(2,1)}, bf16[288,2048]{1,0:T(8,128)(2,1)S(1)}, u32[]{:S(2)}, u32[]{:S(2)}) collective-permute-start(bf16[288,2048]{1,0:T(8,128)(2,1)} %get-tuple-element.20.refs_3_.refs_2_), channel_id=1, source_target_pairs={{2,0},{4,2},{6,4},{7,6},{5,7},{3,5},{1,3},{0,1},{10,8},{12,10},{14... | collective-permute-start | bytes 3538952 | tf_op jit(solution)/shard_map/ppermute | solution.py:619
  160.1 40.9 %collective-permute-start.2 = (bf16[288,2048]{1,0:T(8,128)(2,1)}, bf16[288,2048]{1,0:T(8,128)(2,1)}, u32[]{:S(2)}, u32[]{:S(2)}) collective-permute-start(bf16[288,2048]{1,0:T(8,128)(2,1)} %get-tuple-element.21.refs_4_.refs_8_.refs_7_), channel_id=1, source_target_pairs={{0,2},{2,4},{4,6},{6,7},{7,5},{5,3},{3,1},{1,0},{8,10},{10,12},{12... | collective-permute-start | bytes 3538952 | tf_op jit(solution)/shard_map/ppermute | solution.py:619
  162.1 52.4 %collective-permute-start = (bf16[288,2048]{1,0:T(8,128)(2,1)}, bf16[288,2048]{1,0:T(8,128)(2,1)}, u32[]{:S(2)}, u32[]{:S(2)}) collective-permute-start(bf16[288,2048]{1,0:T(8,128)(2,1)} %get-tuple-element.19.refs_2_.refs_1_), channel_id=1, source_target_pairs={{2,0},{4,2},{6,4},{7,6},{5,7},{3,5},{1,3},{0,1},{10,8},{12,10},{14... | collective-permute-start | bytes 3538952 | tf_op jit(solution)/shard_map/ppermute | solution.py:619
  162.2 52.4 %collective-permute-start.5 = (bf16[288,2048]{1,0:T(8,128)(2,1)}, bf16[288,2048]{1,0:T(8,128)(2,1)}, u32[]{:S(2)}, u32[]{:S(2)}) collective-permute-start(bf16[288,2048]{1,0:T(8,128)(2,1)} %get-tuple-element.22.refs_5_.refs_9_.refs_8_), channel_id=1, source_target_pairs={{0,2},{2,4},{4,6},{6,7},{7,5},{5,3},{3,1},{1,0},{8,10},{10,12},{12... | collective-permute-start | bytes 3538952 | tf_op jit(solution)/shard_map/ppermute | solution.py:619
  167.2 1.1 copy-start.6
  168.2 0.9 copy-start.7
  169.1 1.6 copy-start.8
  170.7 1.3 copy-start.9
  172.0 0.8 copy-start.10
  172.8 7.7 %copy-start.2 = (bf16[288,2048]{1,0:T(8,128)(2,1)S(1)}, bf16[288,2048]{1,0:T(8,128)(2,1)}, u32[]{:S(2)}) copy-start(bf16[288,2048]{1,0:T(8,128)(2,1)} %get-tuple-element.21.refs_4_.refs_8_.refs_7_) | copy-start | bytes 3538948
  172.8 7.7 %copy-start.3 = (bf16[288,2048]{1,0:T(8,128)(2,1)S(1)}, bf16[288,2048]{1,0:T(8,128)(2,1)}, u32[]{:S(2)}) copy-start(bf16[288,2048]{1,0:T(8,128)(2,1)} %get-tuple-element.22.refs_5_.refs_9_.refs_8_) | copy-start | bytes 3538948
  172.9 7.7 %copy-start.4 = (bf16[288,2048]{1,0:T(8,128)(2,1)S(1)}, bf16[288,2048]{1,0:T(8,128)(2,1)}, u32[]{:S(2)}) copy-start(bf16[288,2048]{1,0:T(8,128)(2,1)} %get-tuple-element.19.refs_2_.refs_1_) | copy-start | bytes 3538948
  172.9 7.7 %copy-start.5 = (bf16[288,2048]{1,0:T(8,128)(2,1)S(1)}, bf16[288,2048]{1,0:T(8,128)(2,1)}, u32[]{:S(2)}) copy-start(bf16[288,2048]{1,0:T(8,128)(2,1)} %get-tuple-element.20.refs_3_.refs_2_) | copy-start | bytes 3538948
  179.0 1.6 copy-start.1
  201.0 65.0 %collective-permute-start.3 = (bf16[288,2048]{1,0:T(8,128)(2,1)}, bf16[288,2048]{1,0:T(8,128)(2,1)S(1)}, u32[]{:S(2)}, u32[]{:S(2)}) collective-permute-start(bf16[288,2048]{1,0:T(8,128)(2,1)} %collective-permute-done.2.refs_6_.refs_5_.refs_3_), channel_id=1, source_target_pairs={{0,2},{2,4},{4,6},{6,7},{7,5},{5,3},{3,1},{1,0},{8,10},{10,12},{12... | collective-permute-start | bytes 3538952 | tf_op jit(solution)/shard_map/ppermute | solution.py:619
  201.1 64.9 %collective-permute-start.4 = (bf16[288,2048]{1,0:T(8,128)(2,1)S(1)}, bf16[288,2048]{1,0:T(8,128)(2,1)S(1)}, u32[]{:S(2)}, u32[]{:S(2)}) collective-permute-start(bf16[288,2048]{1,0:T(8,128)(2,1)S(1)} %collective-permute-done.1.refs_5_.refs_4_.refs_2_), channel_id=1, source_target_pairs={{2,0},{4,2},{6,4},{7,6},{5,7},{3,5},{1,3},{0,1},{10,8},{12,10},{14... | collective-permute-start | bytes 3538952 | tf_op jit(solution)/shard_map/ppermute | solution.py:619
where the time goes:
time: 279 us
  Pallas kernels  248 us (89%)
  local copies, waits for them, and re-layouts  12.1 us (4%)
  waiting for transfers between devices  11.5 us (4%)
  starting transfers between devices  6.16 us (2%)
    pallas_call x1, Pallas kernels, exchange(): pl.pallas_call(functools.partial(exchange_kernel, n_row, n_col, parts), i...  143 us
    pallas_call x5, Pallas kernels, tile_job(): pl.pallas_call(functools.partial(tile_kernel, wants, sources, width, firs...  84.3 us
    pallas_call x1, Pallas kernels, whiten_rows(): pl.pallas_call(whiten_kernel, grid=(total // width,), in_specs=[pl.BlockS...  13.8 us
    ppermute x6, waiting for transfers between devices, hop(): return lax.ppermute(a, 'col', perm)  11.5 us
    unnamed x24, local copies, waits for them, and re-layouts  7.27 us
    ppermute x6, starting transfers between devices, hop(): return lax.ppermute(a, 'col', perm)  6.16 us
    pallas_call x1, Pallas kernels, products_job(): pl.pallas_call(products_kernel, in_specs=[smem] * 3 + [vmem] * 6, out_spe...  6.11 us
  transfers between devices with their start and end apart: 6, of which 2 were waited for; matrix products, arithmetic and copies ran while one was open for 1% of the time, Pallas kernels for 28%

commit v1 on v0

--- a/solution.py
+++ b/solution.py
@@ -72,6 +72,13 @@
     return i + mask * (1 - 2 * ((i // mask) % 2))
 
 
+def xor_all(i, mask, n):
+    for m in masks_of(n):
+        if mask & m:
+            i = xor(i, m)
+    return i
+
+
 def split3(x):
     a = x.astype(jnp.bfloat16)
     rest = x - a.astype(jnp.float32)
@@ -88,34 +95,25 @@
     return x[:, 2 * n :] + x[:, n : 2 * n] + x[:, :n]
 
 
-def whiten_kernel(d_ref, dp_ref, f_ref, fp_ref, ac_ref, ar_ref, arp_ref, dir_ref, w_ref, v_ref):
+def whiten_kernel(d_ref, dp_ref, f_ref, fp_ref, ar_ref, arp_ref, w_ref):
     b = pl.program_id(0)
     width = f_ref.shape[0]
     zero = jnp.zeros((width, width), jnp.float32)
     k = lax.broadcasted_iota(jnp.int32, (width, width), 0)
     j = lax.broadcasted_iota(jnp.int32, (width, width), 1)
-    keep = (k > j) & (ac_ref[...] == ar_ref[...])
-    keep_prev = (ac_ref[...] == arp_ref[...]) & (b > 0)
+    column = jnp.broadcast_to(ar_ref[...], (128, width)).T[:, :1]
+    keep = (k > j) & (column == ar_ref[...])
+    keep_prev = (column == arp_ref[...]) & (b > 0)
     here = jnp.where(keep, f_ref[...].astype(jnp.float32), zero).astype(jnp.bfloat16)
     prev = jnp.where(keep_prev, fp_ref[...].astype(jnp.float32), zero).astype(jnp.bfloat16)
     mixed = lax.dot_general(d_ref[...], here, NT, preferred_element_type=jnp.float32)
     mixed += lax.dot_general(dp_ref[...], prev, NT, preferred_element_type=jnp.float32)
-    out = (d_ref[...].astype(jnp.float32) + mixed).astype(jnp.bfloat16)
-    w_ref[...] = out
-    v_ref[...] = fold3(
-        lax.dot_general(
-            out,
-            wide3(dir_ref[...]),
-            (((0,), (0,)), ((), ())),
-            preferred_element_type=jnp.float32,
-        )
-    )
-
-
-def whiten_rows(design, arc_filter, arc_of_row, directions):
+    w_ref[...] = (d_ref[...].astype(jnp.float32) + mixed).astype(jnp.bfloat16)
+
+
+def whiten_rows(design, arc_filter, arc_of_row):
     own, total = design.shape
     width = total // 4
-    cols = directions.shape[1]
     here = lambda b: (0, b)
     prev = lambda b: (0, jnp.maximum(b - 1, 0))
     row = arc_of_row.reshape(1, total)
@@ -127,40 +125,36 @@
             pl.BlockSpec((own, width), prev),
             pl.BlockSpec((width, width), lambda b: (b, b)),
             pl.BlockSpec((width, width), lambda b: (b, jnp.maximum(b - 1, 0))),
-            pl.BlockSpec((width, 1), lambda b: (b, 0)),
             pl.BlockSpec((1, width), here),
             pl.BlockSpec((1, width), prev),
-            pl.BlockSpec((own, cols), lambda b: (0, 0)),
         ],
-        out_specs=[
-            pl.BlockSpec((own, width), here),
-            pl.BlockSpec((width, cols), lambda b: (b, 0)),
-        ],
-        out_shape=[
-            jax.ShapeDtypeStruct((own, total), jnp.bfloat16),
-            jax.ShapeDtypeStruct((total, cols), jnp.float32),
-        ],
+        out_specs=pl.BlockSpec((own, width), here),
+        out_shape=jax.ShapeDtypeStruct((own, total), jnp.bfloat16),
         name="whiten",
         cost_estimate=pl.CostEstimate(
             flops=4 * own * total * width, bytes_accessed=8 * own * total, transcendentals=0
         ),
-    )(design, design, arc_filter, arc_filter, arc_of_row.reshape(total, 1), row, row, directions)
+    )(design, design, arc_filter, arc_filter, row, row)
 
 
 def masks_of(n):
     return [1 << i for i in range(n.bit_length() - 1)]
 
 
-def exchange_kernel(n_row, n_col, parts, w_ref, t_ref, d_ref, v_ref, *refs):
-    rows_ref, up1, up2a, up2b, dn1, dn2a, dn2b, terr_ref, edge_ref, vout = refs[:10]
-    stage, got, acc, s_loc, s_ring, r_ring, s_row, r_row, s_terr, r_terr, s_v, r_v, s_e, r_e = refs[10:]
+def exchange_kernel(n_row, n_col, parts, w_ref, t_ref, d_ref, *refs):
+    rows_ref, up1, up2a, up2b, dn1, dn2a, dn2b, terr_ref, edge_ref, side_ref, pre_ref, vout = refs[:12]
+    b_ref, a_ref, o_ref, got, acc = refs[12:17]
+    s_loc, s_ring, r_ring, s_row, r_row, s_terr, r_terr, s_v, r_v, s_e, r_e = refs[17:]
     r = lax.axis_index("row")
     c = lax.axis_index("col")
-    own = w_ref.shape[0]
+    own, width = w_ref.shape
     sub = own // parts
     zs = n_col // 2
     z, y = c // 2, c % 2
     place = z + y * (n_col - 1 - 2 * z)
+    by_up = place % zs == 0
+    by_down = place % zs == zs - 1
+    inner = (place % zs > 0) & (place % zs < zs - 1)
 
     def col_at(p):
         side = p // zs
@@ -168,9 +162,10 @@
 
     nxt = col_at((place + 1) % n_col)
     prv = col_at((place + n_col - 1) % n_col)
-    row_masks, col_masks = masks_of(n_row), masks_of(n_col)
+    row_masks = masks_of(n_row)
     peers = [(r, nxt), (r, prv)]
-    peers += [(xor(r, m), c) for m in row_masks] + [(r, xor(c, m)) for m in col_masks]
+    peers += [(xor(r, m), c) for m in row_masks] + [(r, xor(c, 1))]
+    peers += [(r, 2 * xor_all(z, m, zs) + y) for m in range(1, zs)]
     barrier = pltpu.get_barrier_semaphore()
     for peer in peers:
         pl.semaphore_signal(barrier, inc=1, device_id=peer, device_id_type=MESH)
@@ -185,8 +180,15 @@
     def piece(ref, j):
         return ref.at[pl.ds(j * sub, sub)]
 
+    sends = []
+
+    def start(copy):
+        copy.start()
+        sends.append(copy)
+
     steps = 2 * parts
     half = parts // 2
+    ahead = 4
 
     def ring(s, way):
         one, two = ((up1, (up2a, up2b)), (dn1, (dn2a, dn2b)))[way]
@@ -198,12 +200,14 @@
         return remote(src, dst, s_ring.at[way, s], r_ring.at[way, s], (r, (nxt, prv)[way]))
 
     rings = [[ring(s, way) for way in range(2)] for s in range(steps)]
-
-    sends = []
-
-    def start(copy):
-        copy.start()
-        sends.append(copy)
+    for s in range(ahead):
+        for way in range(2):
+            start(rings[s][way])
+
+    mine = pl.ds(pl.multiple_of(y * own, own), own)
+    other = pl.ds(pl.multiple_of((1 - y) * own, own), own)
+    load = pltpu.make_async_copy(w_ref, b_ref.at[mine], s_loc.at[0])
+    load.start()
 
     far = n_col // 2
 
@@ -216,121 +220,201 @@
     terrs = {}
     for k in range(1, far + 1):
         terrs[k] = [terr(k, 0)] + ([terr(k, 1)] if k < far else [])
-
-    total = v_ref.shape[0]
-    levels = [("row", m) for m in row_masks] + [("col", m) for m in col_masks]
-    span = total
-    offset = 0
-    gives, keeps, backs, spots = [], [], [], []
-    base = 0
-    for i, (axis, m) in enumerate(levels):
-        at = r if axis == "row" else c
-        peer = (xor(r, m), c) if axis == "row" else (r, xor(c, m))
-        bit = (at // m) % 2
+    for copy in terrs[1]:
+        start(copy)
+    edge = edge_ref.shape[0]
+    edge_at = pl.ds(pl.multiple_of((1 - y) * (own - edge), edge), edge)
+    edges = remote(d_ref.at[edge_at], edge_ref, s_e.at[0], r_e.at[0], (r, xor(c, 1)))
+    start(edges)
+    across = remote(w_ref, side_ref, s_e.at[1], r_e.at[1], (r, xor(c, 1)))
+
+    @pl.when(inner)
+    def _():
+        across.start()
+
+    order = []
+    for mask in reversed(row_masks):
+        for m in range(0, n_row, 2 * mask):
+            order.append((m + mask, mask))
+
+    def row_copy(key, j):
+        m, mask = key
+        n = order.index(key)
+        src = w_ref if m == mask else rows_ref.at[m - mask]
+        return remote(piece(src, j), piece(rows_ref.at[m], j), s_row.at[n, j], r_row.at[n, j],
+                      (xor(r, mask), c))
+
+    copies = {key: [row_copy(key, j) for j in range(parts)] for key in order}
+    filled = {m: (m, mask) for m, mask in order}
+    later = [key for key in order if key[0] != key[1]]
+    waited = set()
+
+    def row_wait(key, j):
+        if (key, j) not in waited:
+            copies[key][j].wait_recv()
+            waited.add((key, j))
+
+    load.wait()
+    put = pltpu.make_async_copy(b_ref.at[mine], rows_ref.at[0], s_loc.at[1])
+    put.start()
+    dirs = wide3(d_ref[...])
+    chunk = width // 8
+
+    @pl.loop(0, 8)
+    def _(t):
+        span = pl.ds(pl.multiple_of(t * chunk, chunk), chunk)
+        acc[span, :] = fold3(
+            lax.dot_general(
+                b_ref[mine, span], dirs, (((0,), (0,)), ((), ())),
+                preferred_element_type=jnp.float32,
+            )
+        )
+
+    levels = [((xor(r, m), c), (r // m) % 2) for m in row_masks] + [((r, xor(c, 1)), y)]
+    n = len(levels)
+    span = width
+    offset = base = 0
+    gives, keeps, spots = [], [], []
+    for i, (peer, bit) in enumerate(levels):
         span //= 2
         give = pl.ds(pl.multiple_of(offset + (1 - bit) * span, span), span)
         offset = offset + bit * span
         keep = pl.ds(pl.multiple_of(offset, span), span)
-        src = (v_ref if i == 0 else acc).at[give]
         spot = pl.ds(base, span)
         base += span
-        gives.append(remote(src, got.at[spot], s_v.at[i], r_v.at[i], peer))
-        n = len(levels)
-        backs.append(remote(vout.at[keep], vout.at[keep], s_v.at[n + i], r_v.at[n + i], peer))
+        gives.append(remote(acc.at[give], got.at[spot], s_v.at[i], r_v.at[i], peer))
         keeps.append(keep)
         spots.append(spot)
-
-    def add(i):
+    bit = span // zs
+    at_out = pl.ds(pl.multiple_of(y * span + z * bit, bit), bit)
+    side_out = pl.ds(pl.multiple_of(y * span, span), span)
+    fans, backs = [], []
+    for m in range(1, zs):
+        zz = xor_all(z, m, zs)
+        peer = (r, 2 * zz + y)
+        give = pl.ds(pl.multiple_of(offset + zz * bit, bit), bit)
+        spot = pl.ds(base + (m - 1) * bit, bit)
+        at = n + 2 * m - 2
+        fans.append(remote(acc.at[give], got.at[spot], s_v.at[at], r_v.at[at], peer))
+        backs.append(
+            remote(vout.at[at_out], vout.at[at_out], s_v.at[at + 1], r_v.at[at + 1], peer)
+        )
+    at = n + 2 * zs - 2
+    last = remote(vout.at[side_out], vout.at[side_out], s_v.at[at], r_v.at[at], (r, xor(c, 1)))
+
+    def finish(i):
         gives[i].wait()
-        held = v_ref if i == 0 else acc
-        into = vout if i == len(levels) - 1 else acc
-        into[keeps[i]] = held[keeps[i]] + got[spots[i]]
-
-    chain = []
-    for i in range(len(levels)):
-        chain.append(("give", i))
-    for i in reversed(range(len(levels))):
-        chain.append(("back", i))
-
-    state = [0]
+        acc[keeps[i]] = acc[keeps[i]] + got[spots[i]]
+
+    def fan_in():
+        for copy in fans:
+            copy.wait()
+        mid = acc[pl.ds(pl.multiple_of(offset + z * bit, bit), bit)]
+        for m in range(1, zs):
+            mid = mid + got[base + (m - 1) * bit : base + m * bit]
+        vout[at_out] = mid
+
+    def each(copies, method):
+        for copy in copies:
+            getattr(copy, method)()
+
+    todo = [lambda: gives[0].start()]
+    for i in range(1, n):
+        todo.append(lambda i=i: (finish(i - 1), gives[i].start()))
+    todo.append(lambda: (finish(n - 1), each(fans, "start")))
+    todo.append(lambda: (fan_in(), each(backs, "start")))
+    todo.append(lambda: (each(backs, "wait"), last.start()))
+    todo.append(lambda: last.wait())
 
     def v_next():
-        at = state[0]
-        if at > len(chain):
-            return
-        if at > 0:
-            kind, i = chain[at - 1]
-            if kind == "give":
-                add(i)
-            else:
-                backs[i].wait()
-        if at < len(chain):
-            kind, i = chain[at]
-            (gives if kind == "give" else backs)[i].start()
-        state[0] = at + 1
-
-    def row_copy(m, mask, j):
-        src = w_ref if m == mask else rows_ref.at[m - mask]
-        n = row_index[(m, mask)]
-        return remote(piece(src, j), piece(rows_ref.at[m], j), s_row.at[n, j], r_row.at[n, j],
-                      (xor(r, mask), c))
-
-    row_index = {}
-    order = []
-    for mask in reversed(row_masks):
-        for m in range(0, n_row, 2 * mask):
-            row_index[(m + mask, mask)] = len(row_index)
-            order.append((m + mask, mask))
+        if todo:
+            todo.pop(0)()
 
     v_next()
-    for copy in terrs[1]:
-        start(copy)
-    for s in range(2):
-        for way in range(2):
-            start(rings[s][way])
-    mine = pltpu.make_async_copy(w_ref, stage, s_loc.at[0])
-    mine.start()
-    edge = edge_ref.shape[0]
-    edge_at = pl.ds(pl.multiple_of((1 - y) * (own - edge), 8), edge)
-    edges = remote(d_ref.at[edge_at], edge_ref, s_e, r_e, (r, xor(c, 1)))
-    start(edges)
     v_next()
-    copies = {key: [row_copy(*key, j) for j in range(parts)] for key in order}
-    first = [key for key in order if key[0] == key[1]]
-    later = [key for key in order if key[0] != key[1]]
-    for key in first:
-        for copy in copies[key]:
-            start(copy)
-    mine.wait()
-    put = pltpu.make_async_copy(stage, rows_ref.at[0], s_loc.at[1])
-    put.start()
+    for key in order:
+        if key[0] == key[1]:
+            for copy in copies[key]:
+                start(copy)
+
+    def other_load(ref):
+        return pltpu.make_async_copy(ref, b_ref.at[other], s_loc.at[2])
+
+    def other_start():
+        @pl.when(inner)
+        def _():
+            across.wait()
+            other_load(side_ref).start()
+
+        @pl.when(by_up)
+        def _():
+            other_load(up1).start()
+
+        @pl.when(by_down)
+        def _():
+            other_load(dn1).start()
+
+    def a_load(m):
+        return pltpu.make_async_copy(rows_ref.at[m], a_ref.at[m % 2], s_loc.at[3 + m % 2])
+
+    def o_store(m):
+        return pltpu.make_async_copy(o_ref.at[m % 2], pre_ref.at[m], s_loc.at[5 + m % 2])
+
+    def own_tile(m):
+        a_load(m).wait()
+        if m == 0:
+            other_load(w_ref).wait()
+        if m >= 2:
+            o_store(m - 2).wait()
+        o_ref[m % 2] = lax.dot_general(
+            a_ref[m % 2], b_ref[...], NT, preferred_element_type=jnp.float32
+        )
+        o_store(m).start()
 
     hop = 1
-    waited = set()
+    lag = parts // 2
+    v_at = [ahead + i * (ahead + 1) for i in range(len(todo))]
     for s in range(steps):
         for way in range(2):
             rings[s][way].wait_recv()
-        if s % 2 == 0 or s > steps - 4:
+        if s in v_at:
             v_next()
-        if s % 2 == 1 and hop <= far:
+        if s % 3 == 2 and hop <= far:
             for copy in terrs[hop]:
                 copy.wait_recv()
             hop += 1
             if hop <= far:
                 for copy in terrs[hop]:
                     start(copy)
-        if s + 2 < steps:
+        if s + ahead < steps:
             for way in range(2):
-                start(rings[s + 2][way])
-        j = s - 2
+                start(rings[s + ahead][way])
+        j = s - lag
         if 0 <= j < parts:
             for key in later:
-                m, mask = key
-                up = [k for k in order if k[0] == m - mask][0]
-                if (up, j) not in waited:
-                    copies[up][j].wait_recv()
-                    waited.add((up, j))
+                row_wait(filled[key[0] - key[1]], j)
                 start(copies[key][j])
+        if s == parts - 1:
+            other_start()
+            put.wait()
+            a_load(0).start()
+        if s == parts + 1:
+            for j in range(parts):
+                row_wait(filled[1], j)
+            a_load(1).start()
+            own_tile(0)
+        if s == parts + 3:
+            own_tile(1)
+        if s == parts + lag:
+            for m in range(2, n_row):
+                for j in range(parts):
+                    row_wait(filled[m], j)
+            a_load(2).start()
+        for m in range(2, n_row):
+            if s == parts + lag + m - 1:
+                if m + 1 < n_row:
+                    a_load(m + 1).start()
+                own_tile(m)
     while hop <= far:
         for copy in terrs[hop]:
             copy.wait_recv()
@@ -338,52 +422,53 @@
         if hop <= far:
             for copy in terrs[hop]:
                 start(copy)
-    while state[0] <= len(chain):
+    while todo:
         v_next()
-    for key in order:
-        for j in range(parts):
-            if (key, j) not in waited:
-                copies[key][j].wait_recv()
     edges.wait_recv()
-    put.wait()
+    for m in (n_row - 2, n_row - 1):
+        o_store(m).wait()
     for copy in sends:
         copy.wait_send()
 
 
-def exchange(n_row, n_col, whitened, terr_stored, directions, partial):
+def exchange(n_row, n_col, whitened, terr_stored, directions):
     own, total = whitened.shape
     cols = directions.shape[1]
     block = terr_stored.shape[1]
-    parts = 6
+    parts = 12
     far = n_col // 2
     any_spec = pl.BlockSpec(memory_space=pl.ANY)
     vmem = pl.BlockSpec(memory_space=pltpu.VMEM)
     whole = jax.ShapeDtypeStruct((own, total), jnp.bfloat16)
     part = jax.ShapeDtypeStruct((own // 2, total), jnp.bfloat16)
-    levels = n_row.bit_length() + n_col.bit_length() - 2
+    levels = n_row.bit_length() + n_col
     moves = n_row - 1
     dma = pltpu.SemaphoreType.DMA
     return pl.pallas_call(
         functools.partial(exchange_kernel, n_row, n_col, parts),
-        in_specs=[any_spec, any_spec, any_spec, vmem],
-        out_specs=[any_spec] * 9 + [vmem],
+        in_specs=[any_spec, any_spec, vmem],
+        out_specs=[any_spec] * 11 + [vmem],
         out_shape=[
             jax.ShapeDtypeStruct((n_row, own, total), jnp.bfloat16),
             whole, part, part, whole, part, part,
             jax.ShapeDtypeStruct((n_col, own, block), jnp.bfloat16),
             jax.ShapeDtypeStruct((block // 2, cols), jnp.float32),
-            jax.ShapeDtypeStruct((total, cols), jnp.float32),
+            whole,
+            jax.ShapeDtypeStruct((n_row, own, 2 * own), jnp.float32),
+            jax.ShapeDtypeStruct((total // n_row, cols), jnp.float32),
         ],
         scratch_shapes=[
-            pltpu.VMEM((own, total), jnp.bfloat16),
+            pltpu.VMEM((2 * own, total), jnp.bfloat16),
+            pltpu.VMEM((2, own, total), jnp.bfloat16),
+            pltpu.VMEM((2, own, 2 * own), jnp.float32),
             pltpu.VMEM((total, cols), jnp.float32),
             pltpu.VMEM((total, cols), jnp.float32),
-            dma((2,)),
+            dma((7,)),
             dma((2, 2 * parts)), dma((2, 2 * parts)),
             dma((moves, parts)), dma((moves, parts)),
             dma((2, far)), dma((2, far)),
-            dma((2 * levels,)), dma((2 * levels,)),
-            dma(()), dma(()),
+            dma((levels,)), dma((levels,)),
+            dma((2,)), dma((2,)),
         ],
         name="exchange",
         compiler_params=pltpu.CompilerParams(
@@ -392,11 +477,12 @@
         cost_estimate=pl.CostEstimate(
             flops=1000000, bytes_accessed=40 * own * total, transcendentals=0
         ),
-    )(whitened, terr_stored, directions, partial)
-
-
-def products_kernel(order_ref, spot_ref, s_ref, t0_ref, t_ref, w_ref, v_ref, d_ref, e_ref,
-                    p_ref, o_ref, inv_ref):
+    )(whitened, terr_stored, directions)
+
+
+def products_kernel(order_ref, spot_ref, s_ref, t0_ref, t_ref, w_ref, d_ref, e_ref, *refs):
+    v_refs = refs[:-3]
+    p_ref, o_ref, inv_ref = refs[-3:]
     own, span = o_ref.shape
     half = e_ref.shape[0]
     block = 2 * half
@@ -409,9 +495,11 @@
 
     side = s_ref[1]
     o_ref[...] = jnp.zeros(o_ref.shape, o_ref.dtype)
-    p_ref[...] = fold3(
-        jnp.dot(w_ref[...], wide3(v_ref[...]), preferred_element_type=jnp.float32)
-    )
+    for m, v_ref in enumerate(v_refs):
+        size = v_ref.shape[0]
+        part = w_ref[:, pl.ds(pl.multiple_of(s_ref[2 + m], size), size)]
+        term = fold3(jnp.dot(part, wide3(v_ref[...]), preferred_element_type=jnp.float32))
+        p_ref[...] = p_ref[...] + term if m else term
     k = lax.broadcasted_iota(jnp.int32, (block, block), 0)
     j = lax.broadcasted_iota(jnp.int32, (block, block), 1)
 
@@ -453,14 +541,14 @@
                     )
 
 
-def products_job(order, spots, scalars, terr_stored, terr_all, whitened, v, directions, edge):
+def products_job(order, spots, scalars, terr_stored, terr_all, whitened, directions, edge, v):
     own = whitened.shape[0]
     cols = directions.shape[1]
     vmem = pl.BlockSpec(memory_space=pltpu.VMEM)
     smem = pl.BlockSpec(memory_space=pltpu.SMEM)
     return pl.pallas_call(
         products_kernel,
-        in_specs=[smem] * 3 + [vmem] * 6,
+        in_specs=[smem] * 3 + [vmem] * (5 + len(v)),
         out_specs=[vmem] * 2,
         out_shape=[
             jax.ShapeDtypeStruct((own, cols), jnp.float32),
@@ -472,17 +560,21 @@
         cost_estimate=pl.CostEstimate(
             flops=6 * own * whitened.shape[1] * cols, bytes_accessed=10000000, transcendentals=0
         ),
-    )(order, spots, scalars, terr_stored, terr_all, whitened, v, directions, edge)
-
-
-def tile_kernel(wants, sources, width, first, terr, s_ref, *refs):
+    )(order, spots, scalars, terr_stored, terr_all, whitened, directions, edge, *v)
+
+
+def tile_kernel(wants, sources, width, first, carry, terr, s_ref, *refs):
     n = 1 + max(at for pair in sources.values() for at, _ in pair)
     bufs = refs[:n]
     a_ref = refs[n]
     rest = refs[n + 1 :]
     if terr:
         t_ref, rest = rest[0], rest[1:]
-    o_hbm, b_ref, o_ref, sem, o_sem = rest if first else rest[1:]
+    if carry:
+        pre_ref, rest = rest[0], rest[1:]
+    if not first:
+        rest = rest[1:]
+    o_hbm, b_ref, o_ref, sem, o_sem = rest[:5]
     i = pl.program_id(0)
     steps = pl.num_programs(0)
     own = a_ref.shape[1]
@@ -532,27 +624,53 @@
     def _():
         out(i - 2, slot).wait()
 
+    if carry:
+        q_ref, q_in, q_out = rest[5:]
+
+        def pull(n):
+            return pltpu.make_async_copy(pre_ref.at[carry[n]], q_ref.at[n], q_in.at[n])
+
+        def push(n):
+            return pltpu.make_async_copy(
+                q_ref.at[n],
+                o_hbm.at[
+                    pl.ds(pl.multiple_of(s_ref[6 + carry[n]] * own, own), own),
+                    pl.ds(pl.multiple_of(s_ref[3] * span, span), span),
+                ],
+                q_out.at[n],
+            )
+
+        @pl.when(i == 0)
+        def _():
+            for n in range(len(carry)):
+                pull(n).start()
+
+        for n in range(len(carry)):
+
+            @pl.when(i == 1 + n)
+            def _():
+                pull(n).wait()
+                if terr and carry[n] == 0:
+                    q_ref[n] += t_ref[...]
+                push(n).start()
+
     o_ref[slot] = lax.dot_general(
         a_ref[0],
         b_ref[pl.ds(pl.multiple_of(lo, 128), width), :],
         NT,
         preferred_element_type=jnp.float32,
     )
-    if terr:
-
-        @pl.when((i == 0) & (s_ref[3] == 1))
-        def _():
-            o_ref[slot] += t_ref[...]
-
     out(i, slot).start()
 
     @pl.when(i == steps - 1)
     def _():
+        for n in range(len(carry)):
+            push(n).wait()
         out(i - 1, 1 - slot).wait()
         out(i, slot).wait()
 
 
-def tile_job(scalars, wants, cands, bufs, rows, width, terr, out):
+def tile_job(scalars, wants, cands, bufs, rows, width, carry, pre, terr, out):
     count, own, total = rows.shape
     span = 2 * own
     first = not isinstance(out, jax.Array)
@@ -571,9 +689,23 @@
     in_specs = [any_spec] * len(arrays) + [
         pl.BlockSpec((1, own, total), lambda i, s: (i, 0, 0)),
     ]
+    scratch = [
+        pltpu.VMEM((span, total), jnp.bfloat16),
+        pltpu.VMEM((2, own, width), jnp.float32),
+        pltpu.SemaphoreType.DMA((4,)),
+        pltpu.SemaphoreType.DMA((2,)),
+    ]
     if terr is not None:
         operands.append(terr)
         in_specs.append(pl.BlockSpec((own, span), lambda i, s: (0, 0)))
+    if carry:
+        operands.append(pre)
+        in_specs.append(any_spec)
+        scratch += [
+            pltpu.VMEM((len(carry), own, span), jnp.float32),
+            pltpu.SemaphoreType.DMA((len(carry),)),
+            pltpu.SemaphoreType.DMA((len(carry),)),
+        ]
     shape = out
     alias = {}
     if not first:
@@ -582,18 +714,13 @@
         in_specs.append(any_spec)
         shape = jax.ShapeDtypeStruct(out.shape, out.dtype)
     return pl.pallas_call(
-        functools.partial(tile_kernel, wants, sources, width, first, terr is not None),
+        functools.partial(tile_kernel, wants, sources, width, first, carry, terr is not None),
         grid_spec=pltpu.PrefetchScalarGridSpec(
             num_scalar_prefetch=1,
             grid=(count,),
             in_specs=in_specs,
             out_specs=any_spec,
-            scratch_shapes=[
-                pltpu.VMEM((span, total), jnp.bfloat16),
-                pltpu.VMEM((2, own, width), jnp.float32),
-                pltpu.SemaphoreType.DMA((4,)),
-                pltpu.SemaphoreType.DMA((2,)),
-            ],
+            scratch_shapes=scratch,
         ),
         out_shape=shape,
         input_output_aliases=alias,
@@ -607,7 +734,7 @@
 
 
 def ring_body(n_row, n_col, design, arc_filter, arc_of_row, terr_stored, block_order, directions):
-    own, _ = design.shape
+    own, total = design.shape
     block = terr_stored.shape[1]
     r = lax.axis_index("row")
     c = lax.axis_index("col")
@@ -625,9 +752,9 @@
     forward = [(col_of[p], col_of[(p + 1) % n_col]) for p in range(n_col)]
     backward = [(d, s) for s, d in forward]
 
-    whitened, partial = whiten_rows(design, arc_filter, arc_of_row, directions)
-    rows, up1, up2a, up2b, dn1, dn2a, dn2b, terr_all, edge, v = exchange(
-        n_row, n_col, whitened, terr_stored, directions, partial
+    whitened = whiten_rows(design, arc_filter, arc_of_row)
+    rows, up1, up2a, up2b, dn1, dn2a, dn2b, terr_all, edge, _, pre, v = exchange(
+        n_row, n_col, whitened, terr_stored, directions
     )
     bufs = {
         0: [(whitened, 0), (whitened, half)],
@@ -654,44 +781,58 @@
     count = per_pair * zs
     spots = np.array([[(pos_of[d] - pos_of[s]) % n_col for d in range(n_col)] for s in range(n_col)])
     local_order = block_order - r * count
+    pieces = {0: v}
+    for mask in reversed(masks_of(n_row)):
+        for m in list(pieces):
+            pieces[m + mask] = lax.ppermute(pieces[m], "row", [(i, i ^ mask) for i in range(n_row)])
+    firsts = np.zeros((n_row, n_row), np.int32)
+    for i in range(n_row):
+        for m in range(n_row):
+            size = total
+            for mask in masks_of(n_row):
+                size //= 2
+                firsts[i, m] += size * (((i ^ m) // mask) % 2)
     products, terr = products_job(
         local_order,
         jnp.asarray(spots, jnp.int32)[c],
-        jnp.stack([(c // 2) * per_pair, c % 2]).astype(jnp.int32),
-        terr_stored, terr_all, whitened, v, directions, edge,
+        jnp.concatenate([jnp.stack([(c // 2) * per_pair, c % 2]), jnp.asarray(firsts)[r]]),
+        terr_stored, terr_all, whitened, directions, edge,
+        [pieces[m] for m in range(n_row)],
     )
 
     wide = own // 128 * 128
-    table = np.zeros((zs, n_col, 6), np.int32)
+    jobs = zs - 1
+    table = np.zeros((jobs, n_col, 6), np.int32)
     for col in range(n_col):
-        jobs = []
+        todo = []
         for zz in range(zs):
             ks = [(pos_of[2 * zz + yy] - pos_of[col]) % n_col for yy in range(2)]
-            ready = max(min(k, n_col - k) for k in ks)
-            jobs.append((ready, zz, ks))
-        for j, (_, zz, ks) in enumerate(sorted(jobs)):
+            if zz != col // 2:
+                todo.append((max(min(k, n_col - k) for k in ks), zz, ks))
+        for j, (_, zz, ks) in enumerate(sorted(todo)):
             late = ks.index(far) if far in ks else 0
-            table[j, col] = [zz, ks[0], ks[1], int(zz == col // 2), 0, late]
+            table[j, col] = [zz, ks[0], ks[1], col // 2, 0, late]
     row_spots = jnp.bitwise_xor(r, jnp.arange(n_row, dtype=jnp.int32))
     out = jax.ShapeDtypeStruct((n_row * own, n_col * own), jnp.float32)
 
-    def job(j, wants, cands, width, terr, out, spot=None):
+    def job(j, wants, cands, width, out, spot=None, carry=(), terr=None):
         use = table[j].copy()
         if spot is not None:
             use[:, 4] = [spot(late) for late in use[:, 5]]
         scalars = jnp.concatenate([jnp.asarray(use)[c], row_spots])
-        return tile_job(scalars, wants, cands, bufs, rows, width, terr, out)
+        return tile_job(scalars, wants, cands, bufs, rows, width, carry, pre, terr, out)
 
     every = lambda s, y, h: s[5] >= 0
     early = lambda s, y, h: s[5] == 1 - y
     tail = lambda s, y, h: (s[5] == y) | (h == 1 - y)
-    for j in range(zs - 1):
+    for j in range(jobs - 1):
         cands = tuple(sorted(set(table[j, :, 1:3].ravel().tolist())))
-        out = job(j, every, cands, 2 * own, terr, out)
-    cands = set(table[zs - 1, :, 1:3].ravel().tolist())
-    out = job(zs - 1, early, tuple(sorted(cands - {far})), wide, None, out,
+        carry = {0: tuple(range(1, n_row)), 1: (0,)}.get(j, ())
+        out = job(j, every, cands, 2 * own, out, None, carry, terr if j == 1 else None)
+    cands = set(table[jobs - 1, :, 1:3].ravel().tolist())
+    out = job(jobs - 1, early, tuple(sorted(cands - {far})), wide, out,
               lambda late: 0 if late == 1 else 2 * own - wide)
-    out = job(zs - 1, tail, tuple(sorted(cands)), 2 * own - wide, None, out,
+    out = job(jobs - 1, tail, tuple(sorted(cands)), 2 * own - wide, out,
               lambda late: wide if late == 1 else 0)
     return out.reshape(n_row, 1, own, n_col * own), products
 
@@ -706,7 +847,7 @@
     def body(design, arc_filter, arc_of_row, terr_stored, block_order, directions):
         args = (design, arc_filter, arc_of_row, terr_stored, block_order, directions)
         own, block = design.shape[0], terr_stored.shape[1]
-        aligned = own % 192 == 0 and own % block == block // 2 and (2 * own) % 128 == 0
+        aligned = n_row > 2 and own % 192 == 0 and own % block == block // 2 and (2 * own) % 128 == 0
         if power_of_two(n_row) and power_of_two(n_col) and n_col > 6 and aligned:
             return ring_body(n_row, n_col, *args)
         return general_body(*args)

time: 279 us -> 248 us (0.89)
  Pallas kernels: 248 us -> 215 us
  local copies, waits for them, and re-layouts: 12.1 us -> 16.2 us
    pallas_call x5 -> x4, Pallas kernels: 84.3 us -> 62.7 us  [tile_job(): pl.pallas_call(functools.partial(tile_kernel, wants, sources, width, firs...]
    ppermute x6, waiting for transfers between devices: 11.5 us -> 0.02 us  [hop(): return lax.ppermute(a, 'col', perm)]
    ppermute x0 -> x3, waiting for transfers between devices: none -> 8.73 us  [ring_body(): lax.ppermute(pieces[m], 'row', [(i, i ^ mask) for i in range(n_row)])]
    pallas_call x1, Pallas kernels: 13.8 us -> 7.72 us  [whiten_rows(): pl.pallas_call(whiten_kernel, grid=(total // width,), in_specs=[pl.BlockS...]
    unnamed x24 -> x28, local copies, waits for them, and re-layouts: 7.27 us -> 13.4 us
    pallas_call x1, Pallas kernels: 143 us -> 138 us  [exchange(): pl.pallas_call(functools.partial(exchange_kernel, n_row, n_col, parts), i...]
  transfers between devices with their start and end apart: 6 -> 9, of which waited for: 2 -> 2; matrix products, arithmetic and copies ran while one was open for 1% -> 1% of each run, Pallas kernels for 28% -> 23%
where the time goes in v1:
time: 248 us; the launch traced here: 247 us
  Pallas kernels  215 us (87%)
  local copies, waits for them, and re-layouts  16.2 us (7%)
  waiting for transfers between devices  8.74 us (4%)
  starting transfers between devices  6.19 us (2%)
    pallas_call x1, Pallas kernels, exchange(): pl.pallas_call(functools.partial(exchange_kernel, n_row, n_col, parts), i...  138 us
    pallas_call x4, Pallas kernels, tile_job(): pl.pallas_call(functools.partial(tile_kernel, wants, sources, width, firs...  62.7 us
    unnamed x28, local copies, waits for them, and re-layouts  13.4 us
    ppermute x3, waiting for transfers between devices, ring_body(): lax.ppermute(pieces[m], 'row', [(i, i ^ mask) for i in range(n_row)])  8.73 us
    pallas_call x1, Pallas kernels, whiten_rows(): pl.pallas_call(whiten_kernel, grid=(total // width,), in_specs=[pl.BlockS...  7.72 us
    pallas_call x1, Pallas kernels, products_job(): pl.pallas_call(products_kernel, in_specs=[smem] * 3 + [vmem] * (5 + len(v...  6.94 us
  transfers between devices with their start and end apart: 9, of which 2 were waited for; matrix products, arithmetic and copies ran while one was open for 1% of the time, Pallas kernels for 23%

profile of v1, /device:TPU:0, one launch (start us, length us, event | category | flops | bytes accessed | tf_op | source)
XLA Modules:
  0.0 247.2 jit_solution(4005927909244620291)
XLA Ops:
  0.6 7.7 %whiten.1.w_ref = bf16[576,2048]{1,0:T(8,128)(2,1)} custom-call(bf16[576,2048]{1,0:T(8,128)(2,1)} %dp_ref.1, bf16[576,2048]{1,0:T(8,128)(2,1)} %dp_ref.1, bf16[2048,2048]{1,0:T(8,128)(2,1)} %fp_ref.1, bf16[2048,2048]{1,0:T(8,128)(2,1)} %fp_ref.1, s32[1,2048]{1,0:T(1,128)} %bitcast.19, s32[1,2048]{1,0:T(1,128)} %bitcast.20), custom_call_target="tpu_custom_call" | custom-call | flops 2415919104 | bytes 9437184 | tf_op jit(solution)/shard_map/whiten/pallas_call | solution.py:120
  8.3 137.7 %exchange.1 = (bf16[4,576,2048]{2,1,0:T(8,128)(2,1)}, bf16[576,2048]{1,0:T(8,128)(2,1)}, bf16[288,2048]{1,0:T(8,128)(2,1)}, bf16[288,2048]{1,0:T(8,128)(2,1)}, b...) custom-call(bf16[576,2048]{1,0:T(8,128)(2,1)} %whiten.1.w_ref, ...), custom_call_target="tpu_custom_call" | custom-call | flops 1000000 | bytes 47185920 | tf_op jit(solution)/shard_map/exchange/pallas_call | solution.py:447
  146.0 1.6 collective-permute-start.7
  147.6 0.0 collective-permute-start.6
  147.6 2.0 collective-permute-start.2
  149.6 0.0 collective-permute-start
  149.6 0.7 fusion
  150.3 0.7 fusion.2
  151.0 0.1 pad_add_fusion.4
  151.1 8.1 %collective-permute-done.7.refs_2_ = f32[512,256]{1,0:T(8,128)} collective-permute-done((f32[512,256]{1,0:T(8,128)}, f32[512,256]{1,0:T(8,128)}, u32[]{:S(2)}, u32[]{:S(2)}) %collective-permute-start.7) | collective-permute-done | bytes 524320 | tf_op jit(solution)/shard_map/ppermute | solution.py:787
  159.2 1.3 copy-done.1
  160.5 1.3 copy-done.2
  161.7 1.3 copy-done.3
  163.0 1.3 copy-done.5
  164.3 19.5 %shard_map.131.refs_11_ = f32[2304,4608]{1,0:T(8,128)} custom-call(s32[10]{0:T(128)S(1)} %get-tuple-element.30.s_ref, bf16[576,2048]{1,0:T(8,128)(2,1)} %get-tuple-element.15.refs_0_, bf16[288,2048]{1,0:T(8,128)(2,1)S(1)} %copy-done.3, bf16[288,2048]{1,0:T(8,128)(2,1)S(1)} %copy-done.5, bf16[288,2048]{1,0:T(8,128)(2,1)S(1)} %copy-done.1, ...), custom_call_target="tpu_custom_call" | custom-call | flops 10871635968 | bytes 20054016 | tf_op jit(solution)/shard_map/pallas_call | solution.py:716
  183.9 0.1 collective-permute-start.8
  183.9 0.7 fusion.3.spot_ref
  184.6 0.7 fusion.4
  185.3 0.1 pad_add_fusion.3.s_ref
  185.4 0.6 collective-permute-done.8.refs_3_
  186.1 1.7 copy-done
  187.7 1.1 copy-done.8
  188.8 0.9 copy-done.9
  189.7 1.3 copy-done.10
  191.0 1.0 copy-done.11
  192.0 0.8 copy-done.12
  192.8 6.9 %products.1 = (f32[576,256]{1,0:T(8,128)}, f32[576,1152]{1,0:T(8,128)S(1)}) custom-call(s32[36]{0:T(128)S(1)} %broadcast_subtract_fusion.order_ref, s32[8]{0:T(128)S(1)} %fusion.3.spot_ref, s32[6]{0:T(128)S(1)} %pad_add_fusion.3.s_ref, bf16[576,128]{1,0:T(8,128)(2,1)S(1)} %copy-done.9, bf16[8,576,128]{2,1,0:T(8,128)(2,1)S(1)} %copy-done.10, ...), custom_call_target="tpu_custom_call" | custom-call | flops 1811939328 | bytes 10000000 | tf_op jit(solution)/shard_map/products/pallas_call | solution.py:549
  199.8 1.5 copy-done.7
  201.3 2.5 %collective-permute-start.4 = (bf16[288,2048]{1,0:T(8,128)(2,1)S(1)}, bf16[288,2048]{1,0:T(8,128)(2,1)S(1)}, u32[]{:S(2)}, u32[]{:S(2)}) collective-permute-start(bf16[288,2048]{1,0:T(8,128)(2,1)S(1)} %collective-permute-done.1.refs_3_.refs_2_), channel_id=1, source_target_pairs={{2,0},{4,2},{6,4},{7,6},{5,7},{3,5},{1,3},{0,1},{10,8},{12,10},{14... | collective-permute-start | bytes 3538952 | tf_op jit(solution)/shard_map/ppermute | solution.py:746
  203.8 20.2 %shard_map.132.refs_7_ = f32[2304,4608]{1,0:T(8,128)} custom-call(s32[10]{0:T(128)S(1)} %get-tuple-element.32.s_ref, bf16[288,2048]{1,0:T(8,128)(2,1)S(1)} %copy-done.4, bf16[288,2048]{1,0:T(8,128)(2,1)S(1)} %copy-done.6, bf16[288,2048]{1,0:T(8,128)(2,1)S(1)} %collective-permute-done.refs_2_.refs_1_, ...), custom_call_target="tpu_custom_call", output_to_operand_aliasing={{}: (12, {})} | custom-call | flops 10871635968 | bytes 20054016 | tf_op jit(solution)/shard_map/pallas_call | solution.py:716
  224.1 10.4 %shard_map.133.refs_9_ = f32[2304,4608]{1,0:T(8,128)} custom-call(s32[10]{0:T(128)S(1)} %get-tuple-element.31.s_ref, bf16[576,2048]{1,0:T(8,128)(2,1)} %get-tuple-element.15.refs_0_, bf16[288,2048]{1,0:T(8,128)(2,1)S(1)} %collective-permute-done.refs_2_.refs_1_, ...), custom_call_target="tpu_custom_call", output_to_operand_aliasing={{}: (8, {})} | custom-call | flops 4831838208 | bytes 14155776 | tf_op jit(solution)/shard_map/pallas_call | solution.py:716
  234.5 12.5 %shard_map.134 = f32[2304,4608]{1,0:T(8,128)} custom-call(s32[10]{0:T(128)S(1)} %get-tuple-element.33.s_ref, bf16[576,2048]{1,0:T(8,128)(2,1)} %get-tuple-element.15.refs_0_, bf16[288,2048]{1,0:T(8,128)(2,1)S(1)} %collective-permute-done.refs_2_.refs_1_, ...), custom_call_target="tpu_custom_call", output_to_operand_aliasing={{}: (10, {})} | custom-call | flops 6039797760 | bytes 15335424 | tf_op jit(solution)/shard_map/pallas_call | solution.py:716
  (29 shorter events, 0.1 us)
Async XLA Ops:
  146.0 13.2 %collective-permute-start.7 = (f32[512,256]{1,0:T(8,128)}, f32[512,256]{1,0:T(8,128)}, u32[]{:S(2)}, u32[]{:S(2)}) collective-permute-start(f32[512,256]{1,0:T(8,128)} %get-tuple-element.24.refs_0_), channel_id=1, source_target_pairs={{0,16},{8,24},{16,0},{24,8},{1,17},{9,25},{17,1},{25,9},{2,18},{10... | collective-permute-start | bytes 1572872 | tf_op jit(solution)/shard_map/ppermute | solution.py:787
  147.6 36.3 %collective-permute-start.6 = (f32[512,256]{1,0:T(8,128)}, f32[512,256]{1,0:T(8,128)}, u32[]{:S(2)}, u32[]{:S(2)}) collective-permute-start(f32[512,256]{1,0:T(8,128)} %get-tuple-element.24.refs_0_), channel_id=1, source_target_pairs={{0,8},{8,0},{16,24},{24,16},{1,9},{9,1},{17,25},{25,17},{2,10},{10... | collective-permute-start | bytes 1572872 | tf_op jit(solution)/shard_map/ppermute | solution.py:787
  147.6 53.7 %collective-permute-start.1 = (bf16[288,2048]{1,0:T(8,128)(2,1)}, bf16[288,2048]{1,0:T(8,128)(2,1)S(1)}, u32[]{:S(2)}, u32[]{:S(2)}) collective-permute-start(bf16[288,2048]{1,0:T(8,128)(2,1)} %get-tuple-element.17.refs_2_.refs_1_), channel_id=1, source_target_pairs={{2,0},{4,2},{6,4},{7,6},{5,7},{3,5},{1,3},{0,1},{10,8},{12,10},{14... | collective-permute-start | bytes 3538952 | tf_op jit(solution)/shard_map/ppermute | solution.py:746
  147.6 53.7 %collective-permute-start.2 = (bf16[288,2048]{1,0:T(8,128)(2,1)}, bf16[288,2048]{1,0:T(8,128)(2,1)S(1)}, u32[]{:S(2)}, u32[]{:S(2)}) collective-permute-start(bf16[288,2048]{1,0:T(8,128)(2,1)} %get-tuple-element.18.refs_3_.refs_6_), channel_id=1, source_target_pairs={{0,2},{2,4},{4,6},{6,7},{7,5},{5,3},{3,1},{1,0},{8,10},{10,12},{12... | collective-permute-start | bytes 3538952 | tf_op jit(solution)/shard_map/ppermute | solution.py:746
  149.6 54.2 %collective-permute-start = (bf16[288,2048]{1,0:T(8,128)(2,1)}, bf16[288,2048]{1,0:T(8,128)(2,1)S(1)}, u32[]{:S(2)}, u32[]{:S(2)}) collective-permute-start(bf16[288,2048]{1,0:T(8,128)(2,1)} %get-tuple-element.16.refs_1_.refs_0_), channel_id=1, source_target_pairs={{2,0},{4,2},{6,4},{7,6},{5,7},{3,5},{1,3},{0,1},{10,8},{12,10},{14... | collective-permute-start | bytes 3538952 | tf_op jit(solution)/shard_map/ppermute | solution.py:746
  159.2 44.6 %collective-permute-start.5 = (bf16[288,2048]{1,0:T(8,128)(2,1)}, bf16[288,2048]{1,0:T(8,128)(2,1)}, u32[]{:S(2)}, u32[]{:S(2)}) collective-permute-start(bf16[288,2048]{1,0:T(8,128)(2,1)} %get-tuple-element.19.refs_4_.refs_7_), channel_id=1, source_target_pairs={{0,2},{2,4},{4,6},{6,7},{7,5},{5,3},{3,1},{1,0},{8,10},{10,12},{12... | collective-permute-start | bytes 3538952 | tf_op jit(solution)/shard_map/ppermute | solution.py:746
  159.2 1.3 copy-start.1
  160.5 1.3 copy-start.2
  161.7 1.3 copy-start.3
  163.0 1.3 copy-start.5
  164.3 21.1 %copy-start.13 = (s32[36]{0:T(128)S(1)}, s32[36]{0:T(128)}, u32[]{:S(2)}) copy-start(s32[36]{0:T(128)} %param.16) | copy-start | bytes 436
  183.9 2.2 collective-permute-start.8
  186.0 1.7 copy-start
  187.7 1.1 copy-start.8
  188.8 0.9 copy-start.9
  189.7 1.3 copy-start.10
  191.0 1.0 copy-start.11
  192.0 0.8 copy-start.12
  192.8 11.0 %copy-start.4 = (bf16[288,2048]{1,0:T(8,128)(2,1)S(1)}, bf16[288,2048]{1,0:T(8,128)(2,1)}, u32[]{:S(2)}) copy-start(bf16[288,2048]{1,0:T(8,128)(2,1)} %get-tuple-element.16.refs_1_.refs_0_) | copy-start | bytes 3538948
  192.8 11.0 %copy-start.6 = (bf16[288,2048]{1,0:T(8,128)(2,1)S(1)}, bf16[288,2048]{1,0:T(8,128)(2,1)}, u32[]{:S(2)}) copy-start(bf16[288,2048]{1,0:T(8,128)(2,1)} %get-tuple-element.17.refs_2_.refs_1_) | copy-start | bytes 3538948
  199.8 1.5 copy-start.7
  201.3 33.2 %collective-permute-start.3 = (bf16[288,2048]{1,0:T(8,128)(2,1)S(1)}, bf16[288,2048]{1,0:T(8,128)(2,1)S(1)}, u32[]{:S(2)}, u32[]{:S(2)}) collective-permute-start(bf16[288,2048]{1,0:T(8,128)(2,1)S(1)} %collective-permute-done.2.refs_4_.refs_3_.refs_5_), channel_id=1, source_target_pairs={{0,2},{2,4},{4,6},{6,7},{7,5},{5,3},{3,1},{1,0},{8,10},{10,12},{12... | collective-permute-start | bytes 3538952 | tf_op jit(solution)/shard_map/ppermute | solution.py:746
  201.3 33.2 %collective-permute-start.4 = (bf16[288,2048]{1,0:T(8,128)(2,1)S(1)}, bf16[288,2048]{1,0:T(8,128)(2,1)S(1)}, u32[]{:S(2)}, u32[]{:S(2)}) collective-permute-start(bf16[288,2048]{1,0:T(8,128)(2,1)S(1)} %collective-permute-done.1.refs_3_.refs_2_), channel_id=1, source_target_pairs={{2,0},{4,2},{6,4},{7,6},{5,7},{3,5},{1,3},{0,1},{10,8},{12,10},{14... | collective-permute-start | bytes 3538952 | tf_op jit(solution)/shard_map/ppermute | solution.py:746

commit v2 on v1

v2 whole, which is shorter than its diff:
```python
import functools

import jax
import jax.numpy as jnp
from jax import lax
from jax.experimental import pallas as pl
from jax.experimental.pallas import tpu as pltpu
from jax.sharding import PartitionSpec as P


HIGH = lax.Precision.HIGHEST
NT = (((1,), (1,)), ((), ()))
MESH = pl.DeviceIdType.MESH


def dot_high(a, b):
    return jnp.dot(a, b, precision=HIGH, preferred_element_type=jnp.float32)


def whiten(design, arc_filter, arc_of_row):
    positions = jnp.arange(arc_filter.shape[0], dtype=jnp.int32)
    keep_mask = (positions[:, None] > positions[None, :]) & (
        arc_of_row[:, None] == arc_of_row[None, :]
    )
    lower_part = jnp.where(keep_mask, arc_filter, jnp.zeros_like(arc_filter))
    mixed_part = lax.dot_general(design, lower_part, NT, preferred_element_type=jnp.float32)
    return (design.astype(jnp.float32) + mixed_part).astype(jnp.bfloat16)


def general_body(design, arc_filter, arc_of_row, terr_stored, block_order, directions):
    whitened = whiten(design, arc_filter, arc_of_row)
    own_width = whitened.shape[0]
    rows_block, terr_rows = (
        lax.all_gather(whitened, "col", axis=0, tiled=True),
        lax.all_gather(terr_stored, "col", axis=0, tiled=True),
    )
    cols_block = lax.all_gather(whitened, "row", axis=0, tiled=True)
    normal_tile = lax.dot_general(cols_block, rows_block, NT, preferred_element_type=jnp.float32)
    block_size = terr_rows.shape[1]
    span_rows = terr_rows.shape[0]
    group_count = span_rows // block_size
    row_index = lax.axis_index("row")
    col_index = lax.axis_index("col")
    local_order = block_order - row_index * group_count
    selector = (local_order[None, :] == jnp.arange(group_count, dtype=jnp.int32)[:, None]).astype(
        jnp.float32
    )
    stored = terr_rows.astype(jnp.float32).reshape(group_count, block_size, block_size)
    symmetric = jnp.triu(stored) + jnp.swapaxes(jnp.triu(stored, 1), 1, 2)
    ordered = jnp.einsum("qt,tab->qab", selector, symmetric, precision=HIGH).reshape(
        span_rows, block_size
    )
    own_rows = lax.dynamic_slice_in_dim(ordered, col_index * own_width, own_width, 0)
    positions = col_index * own_width + jnp.arange(own_width, dtype=jnp.int32)
    onehot = (
        (positions // block_size)[:, None] == jnp.arange(group_count, dtype=jnp.int32)[None, :]
    ).astype(jnp.float32)
    terr_added = (onehot[:, :, None] * own_rows[:, None, :]).reshape(own_width, span_rows)
    current = lax.dynamic_slice_in_dim(normal_tile, row_index * own_width, own_width, 0)
    normal_tile = lax.dynamic_update_slice_in_dim(
        normal_tile, current + terr_added, row_index * own_width, 0
    )
    tile_rows = normal_tile.shape[0]
    partial_sum = dot_high(normal_tile, lax.all_gather(directions, "col", axis=0, tiled=True))
    products = lax.psum_scatter(partial_sum, "row", scatter_dimension=0, tiled=True)
    normals = normal_tile.reshape(tile_rows // own_width, 1, own_width, span_rows)
    return (normals, products)


def xor(i, mask):
    return i + mask * (1 - 2 * ((i // mask) % 2))


def xor_all(i, mask, n):
    for m in masks_of(n):
        if mask & m:
            i = xor(i, m)
    return i


def split3(x):
    a = x.astype(jnp.bfloat16)
    rest = x - a.astype(jnp.float32)
    b = rest.astype(jnp.bfloat16)
    return a, b, (rest - b.astype(jnp.float32)).astype(jnp.bfloat16)


def wide3(x):
    return jnp.concatenate(split3(x), 1)


def fold3(x):
    n = x.shape[1] // 3
    return x[:, 2 * n :] + x[:, n : 2 * n] + x[:, :n]


def whiten_kernel(d_ref, dp_ref, f_ref, fp_ref, ar_ref, arp_ref, w_ref):
    b = pl.program_id(0)
    width = f_ref.shape[0]
    zero = jnp.zeros((width, width), jnp.float32)
    k = lax.broadcasted_iota(jnp.int32, (width, width), 0)
    j = lax.broadcasted_iota(jnp.int32, (width, width), 1)
    column = jnp.broadcast_to(ar_ref[...], (128, width)).T[:, :1]
    keep = (k > j) & (column == ar_ref[...])
    keep_prev = (column == arp_ref[...]) & (b > 0)
    here = jnp.where(keep, f_ref[...].astype(jnp.float32), zero).astype(jnp.bfloat16)
    prev = jnp.where(keep_prev, fp_ref[...].astype(jnp.float32), zero).astype(jnp.bfloat16)
    mixed = lax.dot_general(d_ref[...], here, NT, preferred_element_type=jnp.float32)
    mixed += lax.dot_general(dp_ref[...], prev, NT, preferred_element_type=jnp.float32)
    w_ref[...] = (d_ref[...].astype(jnp.float32) + mixed).astype(jnp.bfloat16)


def whiten_rows(design, arc_filter, arc_of_row):
    own, total = design.shape
    width = total // 4
    here = lambda b: (0, b)
    prev = lambda b: (0, jnp.maximum(b - 1, 0))
    row = arc_of_row.reshape(1, total)
    return pl.pallas_call(
        whiten_kernel,
        grid=(total // width,),
        in_specs=[
            pl.BlockSpec((own, width), here),
            pl.BlockSpec((own, width), prev),
            pl.BlockSpec((width, width), lambda b: (b, b)),
            pl.BlockSpec((width, width), lambda b: (b, jnp.maximum(b - 1, 0))),
            pl.BlockSpec((1, width), here),
            pl.BlockSpec((1, width), prev),
        ],
        out_specs=pl.BlockSpec((own, width), here),
        out_shape=jax.ShapeDtypeStruct((own, total), jnp.bfloat16),
        name="whiten",
        cost_estimate=pl.CostEstimate(
            flops=4 * own * total * width, bytes_accessed=8 * own * total, transcendentals=0
        ),
    )(design, design, arc_filter, arc_filter, row, row)


def masks_of(n):
    return [1 << i for i in range(n.bit_length() - 1)]


def exchange_kernel(n_row, n_col, parts, w_ref, t_ref, d_ref, *refs):
    rows_ref, up1, up2a, up2b, up3a, dn1, dn2a, dn2b, dn3b = refs[:9]
    terr_ref, edge_ref, side_ref, pre_ref, pre0_ref, pre1_ref, vout = refs[9:16]
    b_ref, b0_ref, b1_ref, a_ref, o_ref, got, acc = refs[16:23]
    s_loc, s_a, s_o, s_ring, r_ring, s_row, r_row, s_terr, r_terr, s_v, r_v, s_e, r_e = refs[23:]
    r = lax.axis_index("row")
    c = lax.axis_index("col")
    own, width = w_ref.shape
    sub = own // parts
    zs = n_col // 2
    z, y = c // 2, c % 2
    place = z + y * (n_col - 1 - 2 * z)
    by_up = place % zs == 0
    by_down = place % zs == zs - 1
    inner = (place % zs > 0) & (place % zs < zs - 1)

    def col_at(p):
        side = p // zs
        return 2 * (p + side * (n_col - 1 - 2 * p)) + side

    nxt = col_at((place + 1) % n_col)
    prv = col_at((place + n_col - 1) % n_col)
    row_masks = masks_of(n_row)
    peers = [(r, nxt), (r, prv)]
    peers += [(xor(r, m), c) for m in row_masks] + [(r, xor(c, 1))]
    peers += [(r, 2 * xor_all(z, m, zs) + y) for m in range(1, zs)]
    barrier = pltpu.get_barrier_semaphore()
    for peer in peers:
        pl.semaphore_signal(barrier, inc=1, device_id=peer, device_id_type=MESH)
    pl.semaphore_wait(barrier, len(peers))

    def remote(src, dst, ssem, rsem, peer):
        return pltpu.make_async_remote_copy(
            src_ref=src, dst_ref=dst, send_sem=ssem, recv_sem=rsem, device_id=peer,
            device_id_type=MESH,
        )

    def piece(ref, j):
        return ref.at[pl.ds(j * sub, sub)]

    sends = []

    def start(copy):
        copy.start()
        sends.append(copy)

    half = parts // 2
    steps = 2 * parts + half
    ahead = 4

    def ring(s, way):
        one, two, three = ((up1, (up2a, up2b), up3a), (dn1, (dn2a, dn2b), dn3b))[way]
        j = s % parts
        if s < parts:
            src, dst = piece(w_ref, j), piece(one, j)
        elif s < 2 * parts:
            src, dst = piece(one, j), piece(two[j // half], j % half)
        else:
            src, dst = piece(two[way], j), piece(three, j)
        return remote(src, dst, s_ring.at[way, s], r_ring.at[way, s], (r, (nxt, prv)[way]))

    rings = [[ring(s, way) for way in range(2)] for s in range(steps)]
    for s in range(ahead):
        for way in range(2):
            start(rings[s][way])

    mine = pl.ds(pl.multiple_of(y * own, own), own)
    other = pl.ds(pl.multiple_of((1 - y) * own, own), own)
    load = pltpu.make_async_copy(w_ref, b_ref.at[mine], s_loc.at[0])
    load.start()

    far = n_col // 2

    def terr(k, way):
        src = t_ref if k == 1 else terr_ref.at[(n_col - k + 1) if way == 0 else k - 1]
        at = (n_col - k) if way == 0 else k
        return remote(src, terr_ref.at[at], s_terr.at[way, k - 1], r_terr.at[way, k - 1],
                      (r, (nxt, prv)[way]))

    terrs = {}
    for k in range(1, far + 1):
        terrs[k] = [terr(k, 0)] + ([terr(k, 1)] if k < far else [])
    for copy in terrs[1]:
        start(copy)
    edge = edge_ref.shape[0]
    edge_at = pl.ds(pl.multiple_of((1 - y) * (own - edge), edge), edge)
    edges = remote(d_ref.at[edge_at], edge_ref, s_e.at[0], r_e.at[0], (r, xor(c, 1)))
    start(edges)
    across = remote(w_ref, side_ref, s_e.at[1], r_e.at[1], (r, xor(c, 1)))

    @pl.when(inner)
    def _():
        across.start()

    order = []
    for mask in reversed(row_masks):
        for m in range(0, n_row, 2 * mask):
            order.append((m + mask, mask))

    def row_copy(key, j):
        m, mask = key
        n = order.index(key)
        src = w_ref if m == mask else rows_ref.at[m - mask]
        return remote(piece(src, j), piece(rows_ref.at[m], j), s_row.at[n, j], r_row.at[n, j],
                      (xor(r, mask), c))

    copies = {key: [row_copy(key, j) for j in range(parts)] for key in order}
    filled = {m: (m, mask) for m, mask in order}
    later = [key for key in order if key[0] != key[1]]
    waited = set()

    def row_wait(key, j):
        if (key, j) not in waited:
            copies[key][j].wait_recv()
            waited.add((key, j))

    load.wait()
    put = pltpu.make_async_copy(b_ref.at[mine], rows_ref.at[0], s_loc.at[1])
    put.start()
    dirs = wide3(d_ref[...])
    chunk = width // 8

    @pl.loop(0, 8)
    def _(t):
        span = pl.ds(pl.multiple_of(t * chunk, chunk), chunk)
        acc[span, :] = fold3(
            lax.dot_general(
                b_ref[mine, span], dirs, (((0,), (0,)), ((), ())),
                preferred_element_type=jnp.float32,
            )
        )

    levels = [((xor(r, m), c), (r // m) % 2) for m in row_masks] + [((r, xor(c, 1)), y)]
    n = len(levels)
    span = width
    offset = base = 0
    gives, keeps, spots = [], [], []
    for i, (peer, bit) in enumerate(levels):
        span //= 2
        give = pl.ds(pl.multiple_of(offset + (1 - bit) * span, span), span)
        offset = offset + bit * span
        keep = pl.ds(pl.multiple_of(offset, span), span)
        spot = pl.ds(base, span)
        base += span
        gives.append(remote(acc.at[give], got.at[spot], s_v.at[i], r_v.at[i], peer))
        keeps.append(keep)
        spots.append(spot)
    bit = span // zs
    at_out = pl.ds(pl.multiple_of(offset + z * bit, bit), bit)
    fans, backs = [], []
    for m in range(1, zs):
        zz = xor_all(z, m, zs)
        peer = (r, 2 * zz + y)
        give = pl.ds(pl.multiple_of(offset + zz * bit, bit), bit)
        spot = pl.ds(base + (m - 1) * bit, bit)
        at = n + 2 * m - 2
        fans.append(remote(acc.at[give], got.at[spot], s_v.at[at], r_v.at[at], peer))
        backs.append(
            remote(vout.at[at_out], vout.at[at_out], s_v.at[at + 1], r_v.at[at + 1], peer)
        )
    at = n + 2 * zs - 2
    wider = [
        remote(vout.at[keeps[i]], vout.at[keeps[i]], s_v.at[at + i], r_v.at[at + i], levels[i][0])
        for i in range(n)
    ]

    def finish(i):
        gives[i].wait()
        acc[keeps[i]] = acc[keeps[i]] + got[spots[i]]

    def fan_in():
        for copy in fans:
            copy.wait()
        mid = acc[pl.ds(pl.multiple_of(offset + z * bit, bit), bit)]
        for m in range(1, zs):
            mid = mid + got[base + (m - 1) * bit : base + m * bit]
        vout[at_out] = mid

    def each(copies, method):
        for copy in copies:
            getattr(copy, method)()

    todo = [lambda: gives[0].start()]
    for i in range(1, n):
        todo.append(lambda i=i: (finish(i - 1), gives[i].start()))
    todo.append(lambda: (finish(n - 1), each(fans, "start")))
    todo.append(lambda: (fan_in(), each(backs, "start")))
    todo.append(lambda: (each(backs, "wait"), wider[n - 1].start()))
    for i in range(n - 1, 0, -1):
        todo.append(lambda i=i: (wider[i].wait(), wider[i - 1].start()))
    todo.append(lambda: wider[0].wait())

    def v_next():
        if todo:
            todo.pop(0)()

    v_next()
    v_next()
    for key in order:
        if key[0] == key[1]:
            for copy in copies[key]:
                start(copy)

    wide = own // 128 * 128
    rest = 2 * own - wide
    near_at = pl.multiple_of(y * (2 * own - wide), 128)
    rest_at = pl.multiple_of((1 - y) * wide, 128)
    up_first = place % zs < zs // 2

    def fill(refs, b, at, n):
        size = own // len(refs)
        return [
            pltpu.make_async_copy(ref, b.at[pl.ds(at + i * size, size)], s_loc.at[n + i])
            for i, ref in enumerate(refs)
        ]

    def other_start():
        start_at = (1 - y) * own

        @pl.when(inner)
        def _():
            across.wait()
            each(fill([side_ref], b_ref, start_at, 2), "start")

        @pl.when(by_up)
        def _():
            each(fill([up1], b_ref, start_at, 2), "start")

        @pl.when(by_down)
        def _():
            each(fill([dn1], b_ref, start_at, 2), "start")

        @pl.when(place % 2 == 0)
        def _():
            each(fill([dn1], b0_ref, y * own, 3), "start")

        @pl.when(place % 2 == 1)
        def _():
            each(fill([up1], b0_ref, y * own, 3), "start")

    def second_start():
        @pl.when(up_first)
        def _():
            each(fill([up2a, up2b], b0_ref, (1 - y) * own, 4), "start")
            each(fill([dn2a, dn2b], b1_ref, 0, 6), "start")

        @pl.when(place % zs >= zs // 2)
        def _():
            each(fill([dn2a, dn2b], b0_ref, (1 - y) * own, 4), "start")
            each(fill([up2a, up2b], b1_ref, 0, 6), "start")

    def a_load(m):
        return pltpu.make_async_copy(rows_ref.at[m], a_ref.at[m], s_a.at[m])

    stores = []

    def dots(m, rows, width, into):
        n = len(stores)
        for store in stores[-2:]:
            store.wait()

        def store(t):
            return pltpu.make_async_copy(
                o_ref.at[t, :, pl.ds(0, width)], into(m + t), s_o.at[n + t]
            )

        @pl.loop(0, 2)
        def _(t):
            o_ref[t, :, :width] = lax.dot_general(
                a_ref[m + t], rows(), NT, preferred_element_type=jnp.float32
            )
            store(t).start()

        stores.extend([store(0), store(1)])

    def own_tile(m):
        for i in range(2):
            a_load(m + i).wait()
        if m == 0:
            each(fill([side_ref], b_ref, 0, 2), "wait")
        dots(m, lambda: b_ref[...], 2 * own, lambda m: pre_ref.at[m])

    def near_tile(m):
        if m == 0:
            each(fill([up1], b0_ref, 0, 3), "wait")
        span = pl.ds(near_at, wide)
        dots(m, lambda: b0_ref[span, :], wide, lambda m: pre0_ref.at[m, :, span])

    def rest_tile(m):
        if m == 0:
            each(fill([up2a, up2b], b0_ref, 0, 4), "wait")
        span = pl.ds(rest_at, rest)
        dots(m, lambda: b0_ref[span, :], rest, lambda m: pre0_ref.at[m, :, span])

    def side_tile(m):
        if m == 0:
            each(fill([up2a, up2b], b1_ref, 0, 6), "wait")
        at = pl.multiple_of(y * (own - wide), own - wide)
        dots(m, lambda: b1_ref[pl.ds(at, wide), :], wide, lambda m: pre1_ref.at[m])

    hop = 1
    lag = parts // 2
    v_at = [ahead + i * (ahead + 1) for i in range(5)] + [steps - 3, steps - 1]
    work = {}
    for m in range(0, n_row, 2):
        work.setdefault(parts + 1 + (lag + 1) * (m // 2), []).append((own_tile, m))
        work.setdefault(2 * parts - 3 + m // 2, []).append((near_tile, m))
        work.setdefault(2 * parts + m // 2, []).append((rest_tile, m))
        work.setdefault(2 * parts + 3 + m // 2, []).append((side_tile, m))
    for s in range(steps):
        for way in range(2):
            rings[s][way].wait_recv()
        if s in v_at:
            v_next()
        if s % 3 == 2 and hop <= far:
            for copy in terrs[hop]:
                copy.wait_recv()
            hop += 1
            if hop <= far:
                for copy in terrs[hop]:
                    start(copy)
        if s + ahead < steps:
            for way in range(2):
                start(rings[s + ahead][way])
        j = s - lag
        if 0 <= j < parts:
            for key in later:
                row_wait(filled[key[0] - key[1]], j)
                start(copies[key][j])
        if s == parts - 1:
            other_start()
            put.wait()
            a_load(0).start()
            for j in range(parts):
                row_wait(filled[1], j)
            a_load(1).start()
        if s == parts + lag - 1:
            for m in range(2, n_row):
                for j in range(parts):
                    row_wait(filled[m], j)
                a_load(m).start()
        if s == 2 * parts - 1:
            second_start()
        for do, m in work.get(s, []):
            do(m)
    while hop <= far:
        for copy in terrs[hop]:
            copy.wait_recv()
        hop += 1
        if hop <= far:
            for copy in terrs[hop]:
                start(copy)
    while todo:
        v_next()
    edges.wait_recv()
    for store in stores[-2:]:
        store.wait()
    for copy in sends:
        copy.wait_send()


def exchange(n_row, n_col, whitened, terr_stored, directions):
    own, total = whitened.shape
    cols = directions.shape[1]
    block = terr_stored.shape[1]
    parts = 12
    far = n_col // 2
    any_spec = pl.BlockSpec(memory_space=pl.ANY)
    vmem = pl.BlockSpec(memory_space=pltpu.VMEM)
    whole = jax.ShapeDtypeStruct((own, total), jnp.bfloat16)
    part = jax.ShapeDtypeStruct((own // 2, total), jnp.bfloat16)
    levels = 2 * n_row.bit_length() + n_col
    moves = n_row - 1
    dma = pltpu.SemaphoreType.DMA
    return pl.pallas_call(
        functools.partial(exchange_kernel, n_row, n_col, parts),
        in_specs=[any_spec, any_spec, vmem],
        out_specs=[any_spec] * 15 + [vmem],
        out_shape=[
            jax.ShapeDtypeStruct((n_row, own, total), jnp.bfloat16),
            whole, part, part, part, whole, part, part, part,
            jax.ShapeDtypeStruct((n_col, own, block), jnp.bfloat16),
            jax.ShapeDtypeStruct((block // 2, cols), jnp.float32),
            whole,
            jax.ShapeDtypeStruct((n_row, own, 2 * own), jnp.float32),
            jax.ShapeDtypeStruct((n_row, own, 2 * own), jnp.float32),
            jax.ShapeDtypeStruct((n_row, own, own // 128 * 128), jnp.float32),
            jax.ShapeDtypeStruct((total, cols), jnp.float32),
        ],
        scratch_shapes=[
            pltpu.VMEM((2 * own, total), jnp.bfloat16),
            pltpu.VMEM((2 * own, total), jnp.bfloat16),
            pltpu.VMEM((own, total), jnp.bfloat16),
            pltpu.VMEM((n_row, own, total), jnp.bfloat16),
            pltpu.VMEM((2, own, 2 * own), jnp.float32),
            pltpu.VMEM((total, cols), jnp.float32),
            pltpu.VMEM((total, cols), jnp.float32),
            dma((8,)),
            dma((n_row,)),
            dma((4 * n_row,)),
            dma((2, 3 * parts)), dma((2, 3 * parts)),
            dma((moves, parts)), dma((moves, parts)),
            dma((2, far)), dma((2, far)),
            dma((levels,)), dma((levels,)),
            dma((2,)), dma((2,)),
        ],
        name="exchange",
        compiler_params=pltpu.CompilerParams(
            collective_id=0, has_side_effects=True, vmem_limit_bytes=60 * 1024 * 1024
        ),
        cost_estimate=pl.CostEstimate(
            flops=1000000, bytes_accessed=40 * own * total, transcendentals=0
        ),
    )(whitened, terr_stored, directions)


def carry_kernel(at, n_row, s_ref, order_ref, t0_ref, t_ref, w_ref, d_ref, e_ref, v_ref, *refs):
    pre_ref, pre0_ref, pre1_ref, p_ref, out_ref, inv_ref, q_ref, q1_ref, pull_sem, push_sem = refs
    own, span = q_ref.shape[1:]
    wide = q1_ref.shape[2]
    half = e_ref.shape[0]
    block = 2 * half
    per = own // half
    count = order_ref.shape[0]
    side = s_ref[at["side"]]
    pair = s_ref[at["pair"]]

    def pull(n):
        src = (pre_ref, pre0_ref, pre1_ref)[n // n_row].at[n % n_row]
        dst = q_ref.at[n] if n < 2 * n_row else q1_ref.at[n - 2 * n_row]
        return pltpu.make_async_copy(src, dst, pull_sem.at[n])

    def push(n):
        kind, m = n // n_row, n % n_row
        zz = s_ref[at["own"] + kind]
        column = zz * span if kind < 2 else zz * span + side * (span - wide)
        src = q_ref.at[n] if kind < 2 else q1_ref.at[m]
        return pltpu.make_async_copy(
            src,
            out_ref.at[
                pl.ds(pl.multiple_of(s_ref[at["rows"] + m] * own, own), own),
                pl.ds(pl.multiple_of(column, 128), span if kind < 2 else wide),
            ],
            push_sem.at[n],
        )

    total = 3 * n_row
    for n in range(total):
        pull(n).start()

    @pl.loop(0, count)
    def _(t):
        inv_ref[order_ref[t] - s_ref[at["first"]]] = t

    def pass_on(lo, hi):
        for n in range(lo, hi):
            pull(n).wait()
            push(n).start()

    size = v_ref.shape[0] // n_row
    for m in range(n_row):
        part = slice(m * size, (m + 1) * size)
        term = fold3(
            jnp.dot(w_ref[:, part], wide3(v_ref[part, :]), preferred_element_type=jnp.float32)
        )
        p_ref[...] = p_ref[...] + term if m else term
        pass_on(1 + 2 * m, 3 + 2 * m)
    pull(0).wait()
    k = lax.broadcasted_iota(jnp.int32, (block, block), 0)
    j = lax.broadcasted_iota(jnp.int32, (block, block), 1)

    def stored(g):
        slot, spot = s_ref[at["spots"] + g // per], g % per
        there = pl.ds(pl.multiple_of(spot * half, half), half)
        return jnp.where(
            slot == 0,
            t0_ref[there, :].astype(jnp.float32),
            t_ref[slot, there, :].astype(jnp.float32),
        )

    edge = e_ref[...]
    for q in range(span // block):
        lo = 2 * q

        @pl.when((lo + 1 >= side * per) & (lo < side * per + per))
        def _(q=q, lo=lo):
            t = inv_ref[pair + q]
            s = jnp.concatenate([stored(2 * t), stored(2 * t + 1)], 0)
            sym = jnp.where(k <= j, s, 0.0) + jnp.where(k < j, s, 0.0).T
            for h in range(2):
                i = lo + h - side * per

                @pl.when((i >= 0) & (i < per))
                def _():
                    mine = pl.ds(pl.multiple_of(i * half, half), half)
                    rows = sym[h * half : (h + 1) * half]
                    q_ref[0, mine, q * block : (q + 1) * block] += rows
                    other = i + 1 - 2 * h
                    inside = (other >= 0) & (other < per)
                    safe = jnp.minimum(jnp.maximum(other, 0), per - 1)
                    beside = d_ref[pl.ds(pl.multiple_of(safe * half, half), half), :]
                    beside = jnp.where(inside, beside, edge)
                    this = d_ref[mine, :]
                    near = jnp.concatenate([beside, this] if h else [this, beside], 0)
                    p_ref[mine, :] += fold3(
                        jnp.dot(
                            rows.astype(jnp.bfloat16), wide3(near),
                            preferred_element_type=jnp.float32,
                        )
                    )

    push(0).start()
    pass_on(1 + 2 * n_row, total)
    for n in range(total):
        push(n).wait()


def carry_job(at, scalars, order, terr_stored, terr_all, whitened, directions, edge, v, pres, out):
    own = whitened.shape[0]
    cols = directions.shape[1]
    n_row = pres[0].shape[0]
    vmem = pl.BlockSpec(memory_space=pltpu.VMEM)
    smem = pl.BlockSpec(memory_space=pltpu.SMEM)
    any_spec = pl.BlockSpec(memory_space=pl.ANY)
    return pl.pallas_call(
        functools.partial(carry_kernel, at, n_row),
        in_specs=[smem] * 2 + [vmem] * 6 + [any_spec] * 3,
        out_specs=[vmem, any_spec],
        out_shape=[jax.ShapeDtypeStruct((own, cols), jnp.float32), out],
        scratch_shapes=[
            pltpu.SMEM((order.shape[0],), jnp.int32),
            pltpu.VMEM((2 * n_row, own, 2 * own), jnp.float32),
            pltpu.VMEM((n_row, own, pres[2].shape[2]), jnp.float32),
            pltpu.SemaphoreType.DMA((3 * n_row,)),
            pltpu.SemaphoreType.DMA((3 * n_row,)),
        ],
        name="carry",
        compiler_params=pltpu.CompilerParams(vmem_limit_bytes=60 * 1024 * 1024),
        cost_estimate=pl.CostEstimate(
            flops=6 * own * whitened.shape[1] * cols, bytes_accessed=60000000, transcendentals=0
        ),
    )(scalars, order, terr_stored, terr_all, whitened, directions, edge, v, *pres)


def tile_kernel(parts, rows_at, s_ref, *refs):
    n = 1 + max(i for _, _, sources, _ in parts for pair in sources.values() for i, _ in pair)
    bufs = refs[:n]
    a_ref, _, o_hbm, b_ref, o_ref, sem, o_sem = refs[n:]
    i = pl.program_id(0)
    steps = pl.num_programs(0)
    own = a_ref.shape[1]
    half = own // 2
    span = b_ref.shape[1]

    def copy(p, k, y, h):
        spot, row = parts[p][2][k][h]
        return pltpu.make_async_copy(
            bufs[spot].at[pl.ds(row, half)],
            b_ref.at[p, pl.ds((2 * y + h) * half, half)],
            sem.at[p, 2 * y + h],
        )

    @pl.when(i == 0)
    def _():
        for p, (at, wants, sources, _) in enumerate(parts):
            for y in range(2):
                for h in range(2):
                    needed = wants(s_ref[at + 4], y, h)
                    for k in sources:

                        @pl.when((s_ref[at + 1 + y] == k) & needed)
                        def _():
                            copy(p, k, y, h).start()

    slot = i % 2

    def outs(i, slot):
        copies = []
        first = 0
        for p, (at, _, _, width) in enumerate(parts):
            copies.append(
                pltpu.make_async_copy(
                    o_ref.at[slot, :, pl.ds(first, width)],
                    o_hbm.at[
                        pl.ds(pl.multiple_of(s_ref[rows_at + i] * own, own), own),
                        pl.ds(pl.multiple_of(s_ref[at] * span + s_ref[at + 3], 128), width),
                    ],
                    o_sem.at[p, slot],
                )
            )
            first += width
        return copies

    @pl.when(i >= 2)
    def _():
        for out in outs(i - 2, slot):
            out.wait()

    first = 0
    for p, (at, wants, sources, width) in enumerate(parts):

        @pl.when(i == 0)
        def _():
            for y in range(2):
                for h in range(2):

                    @pl.when(wants(s_ref[at + 4], y, h))
                    def _():
                        copy(p, next(iter(sources)), y, h).wait()

        o_ref[slot, :, first : first + width] = lax.dot_general(
            a_ref[0],
            b_ref[p, pl.ds(pl.multiple_of(s_ref[at + 3], 128), width), :],
            NT,
            preferred_element_type=jnp.float32,
        )
        outs(i, slot)[p].start()
        first += width

    @pl.when(i == steps - 1)
    def _():
        for out in outs(i - 1, 1 - slot) + outs(i, slot):
            out.wait()


def tile_job(scalars, rows_at, parts, bufs, rows, out):
    count, own, total = rows.shape
    span = 2 * own
    any_spec = pl.BlockSpec(memory_space=pl.ANY)
    arrays, made = [], []
    for at, wants, cands, width in parts:
        sources = {}
        for k in cands:
            pair = []
            for array, row in bufs[k]:
                spot = [i for i, a in enumerate(arrays) if a is array]
                if not spot:
                    arrays.append(array)
                    spot = [len(arrays) - 1]
                pair.append((spot[0], row))
            sources[k] = pair
        made.append((at, wants, sources, width))
    columns = sum(width for *_, width in parts)
    return pl.pallas_call(
        functools.partial(tile_kernel, made, rows_at),
        grid_spec=pltpu.PrefetchScalarGridSpec(
            num_scalar_prefetch=1,
            grid=(count,),
            in_specs=[any_spec] * len(arrays)
            + [pl.BlockSpec((1, own, total), lambda i, s: (i, 0, 0)), any_spec],
            out_specs=any_spec,
            scratch_shapes=[
                pltpu.VMEM((len(parts), span, total), jnp.bfloat16),
                pltpu.VMEM((2, own, columns), jnp.float32),
                pltpu.SemaphoreType.DMA((len(parts), 4)),
                pltpu.SemaphoreType.DMA((len(parts), 2)),
            ],
        ),
        out_shape=jax.ShapeDtypeStruct(out.shape, out.dtype),
        input_output_aliases={2 + len(arrays): 0},
        compiler_params=pltpu.CompilerParams(vmem_limit_bytes=60 * 1024 * 1024),
        cost_estimate=pl.CostEstimate(
            flops=2 * count * own * columns * total,
            bytes_accessed=2 * count * own * total + 4 * count * own * columns,
            transcendentals=0,
        ),
    )(scalars, *arrays, rows, out)


def ring_body(n_row, n_col, design, arc_filter, arc_of_row, terr_stored, block_order, directions):
    own, _ = design.shape
    block = terr_stored.shape[1]
    r = lax.axis_index("row")
    c = lax.axis_index("col")
    zs = n_col // 2
    half = own // 2
    far = n_col // 2

    def hop(a, perm):
        return lax.ppermute(a, "col", perm)

    col_of = [2 * p if p < zs else 2 * (n_col - 1 - p) + 1 for p in range(n_col)]
    pos_of = [0] * n_col
    for p, col in enumerate(col_of):
        pos_of[col] = p
    forward = [(col_of[p], col_of[(p + 1) % n_col]) for p in range(n_col)]
    backward = [(d, s) for s, d in forward]

    whitened = whiten_rows(design, arc_filter, arc_of_row)
    rows, up1, up2a, up2b, up3a, dn1, dn2a, dn2b, dn3b, terr_all, edge, _, *pres, v = exchange(
        n_row, n_col, whitened, terr_stored, directions
    )
    last = far - 1
    bufs = {
        2: [(dn2a, 0), (dn2b, 0)],
        n_col - 2: [(up2a, 0), (up2b, 0)],
        1: [(dn1, 0), (dn1, half)],
        n_col - 1: [(up1, 0), (up1, half)],
    }
    upper = hop(up2b, forward)
    lower = hop(dn2a, backward)
    bufs[n_col - last] = [(up3a, 0), (upper, 0)]
    bufs[last] = [(lower, 0), (dn3b, 0)]
    bufs[far] = [(hop(up3a, forward), 0), (hop(dn3b, backward), 0)]

    per_pair = 2 * own // block

    wide = own // 128 * 128
    names = ["tile1b", "tile2a", "tile2b"]
    by_col, by_row, ks_of = [], [], {name: [set(), set()] for name in names}
    for col in range(n_col):
        z, y = col // 2, col % 2
        line = []
        for name in names:
            zz = z ^ 2 if name == "tile1b" else z ^ 3
            ks = [(pos_of[2 * zz + yy] - pos_of[col]) % n_col for yy in range(2)]
            near = [min(k, n_col - k) for k in ks]
            late = int(near[1] > near[0])
            soon = name[-1] == "a"
            lo = (2 * own - wide) * (1 - late) if soon else wide * late
            line += [zz, ks[0], ks[1], lo, late]
            ks_of[name][0].add(ks[1 - late])
            ks_of[name][1].add(ks[late])
        line += [(pos_of[s] - pos_of[col]) % n_col for s in range(n_col)]
        by_col.append(line + [y, z * per_pair, z, z ^ 1, z ^ 2])
    for row in range(n_row):
        by_row.append([row ^ m for m in range(n_row)] + [row * per_pair * zs])
    scalars = jnp.concatenate(
        [jnp.asarray(by_col, jnp.int32)[c], jnp.asarray(by_row, jnp.int32)[r]]
    )
    at = {"spots": 5 * len(names)}
    at["side"] = at["spots"] + n_col
    at["pair"] = at["side"] + 1
    at["own"] = at["side"] + 2
    at["rows"] = at["side"] + 5
    at["first"] = at["rows"] + n_row

    out = jax.ShapeDtypeStruct((n_row * own, n_col * own), jnp.float32)
    products, out = carry_job(
        at, scalars, block_order, terr_stored, terr_all, whitened, directions, edge,
        v, pres, out,
    )
    early = lambda late, y, h: late == 1 - y
    tail = lambda late, y, h: (late == y) | (h == 1 - y)
    parts = []
    for j, name in enumerate(names):
        soon, late = ks_of[name]
        if name[-1] == "a":
            parts.append((5 * j, early, sorted(soon), wide))
        else:
            parts.append((5 * j, tail, sorted(soon | late), 2 * own - wide))
    for some in (parts[:2], parts[2:]):
        out = tile_job(scalars, at["rows"], some, bufs, rows, out)
    return out.reshape(n_row, 1, own, n_col * own), products


def power_of_two(n):
    return n > 1 and n & (n - 1) == 0


def solution(mesh):
    n_row, n_col = mesh.shape["row"], mesh.shape["col"]

    def body(design, arc_filter, arc_of_row, terr_stored, block_order, directions):
        args = (design, arc_filter, arc_of_row, terr_stored, block_order, directions)
        own, block = design.shape[0], terr_stored.shape[1]
        aligned = n_row > 2 and own % 192 == 0 and own % block == block // 2 and (2 * own) % 128 == 0
        if power_of_two(n_row) and n_col == 8 and aligned:
            return ring_body(n_row, n_col, *args)
        return general_body(*args)

    return jax.shard_map(
        body,
        mesh=mesh,
        in_specs=(
            P(("row", "col"), None),
            P(),
            P(),
            P(("row", "col"), None),
            P("row"),
            P(("row", "col"), None),
        ),
        out_specs=(P(None, "col", None, "row"), P(("row", "col"), None)),
        check_vma=False,
    )
```

time: 248 us -> 241 us (0.972)
  Pallas kernels: 215 us -> 229 us
  local copies, waits for them, and re-layouts: 16.2 us -> 3.74 us
  waiting for transfers between devices: 8.74 us -> 2.47 us
    pallas_call x1, Pallas kernels: 138 us -> 165 us  [exchange(): pl.pallas_call(functools.partial(exchange_kernel, n_row, n_col, parts), i...]
    pallas_call x5 -> x3, Pallas kernels: 69.6 us -> 55.8 us  [the longest x2 33.8 us: tile_job(): pl.pallas_call(functools.partial(tile_kernel, made, rows_at), grid_spec=p...]
    unnamed x28 -> x6, local copies, waits for them, and re-layouts: 13.4 us -> 2.36 us
    ppermute x3 -> x0, waiting for transfers between devices: 8.73 us -> none  [ring_body(): lax.ppermute(pieces[m], 'row', [(i, i ^ mask) for i in range(n_row)])]
  transfers between devices with their start and end apart: 9 -> 4, of which waited for: 2 -> 3; matrix products, arithmetic and copies ran while one was open for 1% -> 1% of each run, Pallas kernels for 23% -> 17%
where the time goes in v2:
time: 241 us; the launch traced here: 240 us
  Pallas kernels  229 us (95%)
  starting transfers between devices  4.1 us (2%)
  local copies, waits for them, and re-layouts  3.74 us (2%)
  waiting for transfers between devices  2.47 us (1%)
    pallas_call x1, Pallas kernels, exchange(): pl.pallas_call(functools.partial(exchange_kernel, n_row, n_col, parts), i...  165 us
    pallas_call x2, Pallas kernels, tile_job(): pl.pallas_call(functools.partial(tile_kernel, made, rows_at), grid_spec=p...  33.8 us
    pallas_call x1, Pallas kernels, carry_job(): pl.pallas_call(functools.partial(carry_kernel, at, n_row), in_specs=[smem...  22 us
    pallas_call x1, Pallas kernels, whiten_rows(): pl.pallas_call(whiten_kernel, grid=(total // width,), in_specs=[pl.BlockS...  7.77 us
  transfers between devices with their start and end apart: 4, of which 3 were waited for; matrix products, arithmetic and copies ran while one was open for 1% of the time, Pallas kernels for 17%

profile of v2, /device:TPU:0, one launch (start us, length us, event | category | flops | bytes accessed | tf_op | source)
XLA Modules:
  0.0 240.3 jit_solution(12586429734306920739)
XLA Ops:
  0.6 7.8 %whiten.1.w_ref = bf16[576,2048]{1,0:T(8,128)(2,1)} custom-call(bf16[576,2048]{1,0:T(8,128)(2,1)} %dp_ref.1, bf16[576,2048]{1,0:T(8,128)(2,1)} %dp_ref.1, bf16[2048,2048]{1,0:T(8,128)(2,1)} %fp_ref.1, bf16[2048,2048]{1,0:T(8,128)(2,1)} %fp_ref.1, s32[1,2048]{1,0:T(1,128)} %bitcast.9, s32[1,2048]{1,0:T(1,128)} %bitcast.10), custom_call_target="tpu_custom_call" | custom-call | flops 2415919104 | bytes 9437184 | tf_op jit(solution)/shard_map/whiten/pallas_call | solution.py:119
  8.4 165.0 %exchange.1 = (bf16[4,576,2048]{2,1,0:T(8,128)(2,1)}, bf16[576,2048]{1,0:T(8,128)(2,1)}, bf16[288,2048]{1,0:T(8,128)(2,1)}, bf16[288,2048]{1,0:T(8,128)(2,1)}, b...) custom-call(bf16[576,2048]{1,0:T(8,128)(2,1)} %whiten.1.w_ref, ...), custom_call_target="tpu_custom_call" | custom-call | flops 1000000 | bytes 47185920 | tf_op jit(solution)/shard_map/exchange/pallas_call | solution.py:517
  173.4 0.1 collective-permute-start
  173.5 2.0 collective-permute-start.3
  175.5 0.0 collective-permute-start.1
  175.5 2.0 collective-permute-start.2
  177.5 0.7 dynamic-slice_bitcast_fusion.1
  178.2 0.7 dynamic-slice_bitcast_fusion
  178.9 0.6 pad_add_fusion.s_ref
  179.5 22.0 %carry.1 = (f32[576,256]{1,0:T(8,128)}, f32[2304,4608]{1,0:T(8,128)}) custom-call(s32[33]{0:T(128)} %pad_add_fusion.s_ref, s32[36]{0:T(128)} %order_ref.1, bf16[576,128]{1,0:T(8,128)(2,1)} %t0_ref.1, bf16[8,576,128]{2,1,0:T(8,128)(2,1)} %get-tuple-element.28.t_ref, bf16[576,2048]{1,0:T(8,128)(2,1)} %whiten.1.w_ref, f32[576,256]{1,0:T(8,128)} %d_ref.5, ...), custom_call_target="tpu_custom_call" | custom-call | flops 1811939328 | bytes 60000000 | tf_op jit(solution)/shard_map/carry/pallas_call | solution.py:667
  201.5 1.0 collective-permute-done.refs_2_.refs_1_
  202.5 0.0 copy-start
  202.5 0.1 collective-permute-done.3.refs_5_.refs_6_
  202.6 0.0 copy-start.1
  202.6 0.9 copy-done
  203.5 0.4 copy-done.1
  204.0 19.8 %shard_map.95.refs_9_ = f32[2304,4608]{1,0:T(8,128)} custom-call(s32[33]{0:T(128)} %pad_add_fusion.s_ref, bf16[288,2048]{1,0:T(8,128)(2,1)} %get-tuple-element.20.refs_0_, bf16[288,2048]{1,0:T(8,128)(2,1)} %get-tuple-element.26.refs_1_, bf16[288,2048]{1,0:T(8,128)(2,1)} %copy-done, ...), custom_call_target="tpu_custom_call", output_to_operand_aliasing={{}: (12, {})} | custom-call | flops 10871635968 | bytes 20054016 | tf_op jit(solution)/shard_map/pallas_call | solution.py:786
  223.8 1.3 collective-permute-done.1.refs_3_
  225.1 0.0 copy-start.2
  225.1 0.0 collective-permute-done.2.refs_4_
  225.1 1.0 copy-done.2
  226.1 14.0 %shard_map.96 = f32[2304,4608]{1,0:T(8,128)} custom-call(s32[33]{0:T(128)} %pad_add_fusion.s_ref, bf16[576,2048]{1,0:T(8,128)(2,1)} %get-tuple-element.19.refs_8_.refs_0_, bf16[288,2048]{1,0:T(8,128)(2,1)} %copy-done, bf16[288,2048]{1,0:T(8,128)(2,1)} %get-tuple-element.21.refs_3_.refs_2_, ...), custom_call_target="tpu_custom_call", output_to_operand_aliasing={{}: (10, {})} | custom-call | flops 6039797760 | bytes 15335424 | tf_op jit(solution)/shard_map/pallas_call | solution.py:786
Async XLA Ops:
  173.4 29.1 %collective-permute-start = (bf16[288,2048]{1,0:T(8,128)(2,1)}, bf16[288,2048]{1,0:T(8,128)(2,1)S(1)}, u32[]{:S(2)}, u32[]{:S(2)}) collective-permute-start(bf16[288,2048]{1,0:T(8,128)(2,1)} %get-tuple-element.20.refs_0_), channel_id=1, source_target_pairs={{2,0},{4,2},{6,4},{7,6},{5,7},{3,5},{1,3},{0,1},{10,8},{12,10},{14... | collective-permute-start | bytes 3538952 | tf_op jit(solution)/shard_map/ppermute | solution.py:822
  173.5 29.1 %collective-permute-start.3 = (bf16[288,2048]{1,0:T(8,128)(2,1)}, bf16[288,2048]{1,0:T(8,128)(2,1)S(1)}, u32[]{:S(2)}, u32[]{:S(2)}) collective-permute-start(bf16[288,2048]{1,0:T(8,128)(2,1)} %get-tuple-element.23.refs_7_), channel_id=1, source_target_pairs={{0,2},{2,4},{4,6},{6,7},{7,5},{5,3},{3,1},{1,0},{8,10},{10,12},{12... | collective-permute-start | bytes 3538952 | tf_op jit(solution)/shard_map/ppermute | solution.py:822
  175.5 49.6 %collective-permute-start.1 = (bf16[288,2048]{1,0:T(8,128)(2,1)}, bf16[288,2048]{1,0:T(8,128)(2,1)S(1)}, u32[]{:S(2)}, u32[]{:S(2)}) collective-permute-start(bf16[288,2048]{1,0:T(8,128)(2,1)} %get-tuple-element.22.refs_4_.refs_5_), channel_id=1, source_target_pairs={{0,2},{2,4},{4,6},{6,7},{7,5},{5,3},{3,1},{1,0},{8,10},{10,12},{12... | collective-permute-start | bytes 3538952 | tf_op jit(solution)/shard_map/ppermute | solution.py:822
  175.5 49.6 %collective-permute-start.2 = (bf16[288,2048]{1,0:T(8,128)(2,1)}, bf16[288,2048]{1,0:T(8,128)(2,1)}, u32[]{:S(2)}, u32[]{:S(2)}) collective-permute-start(bf16[288,2048]{1,0:T(8,128)(2,1)} %get-tuple-element.21.refs_3_.refs_2_), channel_id=1, source_target_pairs={{2,0},{4,2},{6,4},{7,6},{5,7},{3,5},{1,3},{0,1},{10,8},{12,10},{14... | collective-permute-start | bytes 3538952 | tf_op jit(solution)/shard_map/ppermute | solution.py:822
  202.5 1.0 copy-start
  202.6 1.4 copy-start.1
  225.1 1.0 copy-start.2

commit v3 on v2

--- a/solution.py
+++ b/solution.py
@@ -143,8 +143,8 @@
 def exchange_kernel(n_row, n_col, parts, w_ref, t_ref, d_ref, *refs):
     rows_ref, up1, up2a, up2b, up3a, dn1, dn2a, dn2b, dn3b = refs[:9]
     terr_ref, edge_ref, side_ref, pre_ref, pre0_ref, pre1_ref, vout = refs[9:16]
-    b_ref, b0_ref, b1_ref, a_ref, o_ref, got, acc = refs[16:23]
-    s_loc, s_a, s_o, s_ring, r_ring, s_row, r_row, s_terr, r_terr, s_v, r_v, s_e, r_e = refs[23:]
+    b_ref, b0_ref, b1_ref, a_ref, o_ref, got, acc, pack = refs[16:24]
+    s_loc, s_a, s_o, s_ring, r_ring, s_row, r_row, s_terr, r_terr, s_v, r_v, s_e, r_e = refs[24:]
     r = lax.axis_index("row")
     c = lax.axis_index("col")
     own, width = w_ref.shape
@@ -212,9 +212,29 @@
     load.start()
 
     far = n_col // 2
+    h = t_ref.shape[1] // 2
+    pairs = own // h // 2
+    k = lax.broadcasted_iota(jnp.int32, (h, 2 * h), 0)
+    lane = lax.broadcasted_iota(jnp.int32, (h, 2 * h), 1)
+    line = lax.broadcasted_iota(jnp.int32, (16, 2 * h), 0)
+    diagonals = jnp.zeros((16, 2 * h), jnp.float32)
+
+    def stored(i):
+        return t_ref[pl.ds(pl.multiple_of(i * h, h), h), :].astype(jnp.float32)
+
+    for p in range(pairs):
+        top, low = stored(2 * p + y), stored(2 * p + 1 + y)
+        turned = pltpu.roll(jnp.concatenate([top, low], 0).T[h:], h, 1)
+        pack[p * h : (p + 1) * h] = jnp.where(k <= lane, top, turned).astype(pack.dtype)
+        row = jnp.sum(jnp.where(lane == k + h, low, 0.0), axis=0, keepdims=True)
+        diagonals = jnp.where(line == p, row, diagonals)
+    pack[pairs * h : (pairs + 1) * h] = stored(2 * pairs * (1 - y)).astype(pack.dtype)
+    pack[(pairs + 1) * h :] = diagonals.astype(pack.dtype)
+    keep_pack = pltpu.make_async_copy(pack, terr_ref.at[0], s_loc.at[8])
+    keep_pack.start()
 
     def terr(k, way):
-        src = t_ref if k == 1 else terr_ref.at[(n_col - k + 1) if way == 0 else k - 1]
+        src = pack if k == 1 else terr_ref.at[(n_col - k + 1) if way == 0 else k - 1]
         at = (n_col - k) if way == 0 else k
         return remote(src, terr_ref.at[at], s_terr.at[way, k - 1], r_terr.at[way, k - 1],
                       (r, (nxt, prv)[way]))
@@ -495,6 +515,7 @@
     while todo:
         v_next()
     edges.wait_recv()
+    keep_pack.wait()
     for store in stores[-2:]:
         store.wait()
     for copy in sends:
@@ -505,6 +526,7 @@
     own, total = whitened.shape
     cols = directions.shape[1]
     block = terr_stored.shape[1]
+    packed = ((2 * own // block // 2 + 1) * block // 2 + 16, block)
     parts = 12
     far = n_col // 2
     any_spec = pl.BlockSpec(memory_space=pl.ANY)
@@ -516,12 +538,12 @@
     dma = pltpu.SemaphoreType.DMA
     return pl.pallas_call(
         functools.partial(exchange_kernel, n_row, n_col, parts),
-        in_specs=[any_spec, any_spec, vmem],
+        in_specs=[any_spec, vmem, vmem],
         out_specs=[any_spec] * 15 + [vmem],
         out_shape=[
             jax.ShapeDtypeStruct((n_row, own, total), jnp.bfloat16),
             whole, part, part, part, whole, part, part, part,
-            jax.ShapeDtypeStruct((n_col, own, block), jnp.bfloat16),
+            jax.ShapeDtypeStruct((n_col,) + packed, jnp.bfloat16),
             jax.ShapeDtypeStruct((block // 2, cols), jnp.float32),
             whole,
             jax.ShapeDtypeStruct((n_row, own, 2 * own), jnp.float32),
@@ -537,7 +559,8 @@
             pltpu.VMEM((2, own, 2 * own), jnp.float32),
             pltpu.VMEM((total, cols), jnp.float32),
             pltpu.VMEM((total, cols), jnp.float32),
-            dma((8,)),
+            pltpu.VMEM(packed, jnp.bfloat16),
+            dma((9,)),
             dma((n_row,)),
             dma((4 * n_row,)),
             dma((2, 3 * parts)), dma((2, 3 * parts)),
@@ -556,7 +579,7 @@
     )(whitened, terr_stored, directions)
 
 
-def carry_kernel(at, n_row, s_ref, order_ref, t0_ref, t_ref, w_ref, d_ref, e_ref, v_ref, *refs):
+def carry_kernel(at, n_row, s_ref, order_ref, t_ref, w_ref, d_ref, e_ref, v_ref, *refs):
     pre_ref, pre0_ref, pre1_ref, p_ref, out_ref, inv_ref, q_ref, q1_ref, pull_sem, push_sem = refs
     own, span = q_ref.shape[1:]
     wide = q1_ref.shape[2]
@@ -611,14 +634,32 @@
     k = lax.broadcasted_iota(jnp.int32, (block, block), 0)
     j = lax.broadcasted_iota(jnp.int32, (block, block), 1)
 
-    def stored(g):
-        slot, spot = s_ref[at["spots"] + g // per], g % per
-        there = pl.ds(pl.multiple_of(spot * half, half), half)
-        return jnp.where(
-            slot == 0,
-            t0_ref[there, :].astype(jnp.float32),
-            t_ref[slot, there, :].astype(jnp.float32),
+    pairs = per // 2
+    zero = jnp.zeros((half, block), jnp.float32)
+    upper = lax.broadcasted_iota(jnp.int32, (half, block), 0)
+    lane = lax.broadcasted_iota(jnp.int32, (half, block), 1)
+    line = lax.broadcasted_iota(jnp.int32, (16, block), 0)
+
+    def symmetric(t):
+        one, two = 2 * t // per, (2 * t + 1) // per
+        p = 2 * t % per // 2
+        slot = s_ref[at["spots"] + one]
+        split = one != two
+
+        def read(slot, first, n):
+            return t_ref[slot, pl.ds(first, n), :].astype(jnp.float32)
+
+        top = read(slot, pl.multiple_of(p * half, half), half)
+        low = read(s_ref[at["spots"] + two], pairs * half, half)
+        row = jnp.sum(
+            jnp.where(line == p, read(slot, (pairs + 1) * half, 16), 0.0), axis=0, keepdims=True
         )
+        turned = jnp.where((upper > lane) & (lane < half), top, 0.0)
+        turned = jnp.where(split, zero, pltpu.roll(turned, half, 1))
+        s = jnp.concatenate([top, jnp.where(split, low, zero)], 0)
+        strict = jnp.where(k < j, s, 0.0) + jnp.concatenate([zero, turned], 0)
+        diagonal = jnp.where(split | (k < half), s, row)
+        return strict + strict.T + jnp.where(k == j, diagonal, 0.0)
 
     edge = e_ref[...]
     for q in range(span // block):
@@ -626,9 +667,7 @@
 
         @pl.when((lo + 1 >= side * per) & (lo < side * per + per))
         def _(q=q, lo=lo):
-            t = inv_ref[pair + q]
-            s = jnp.concatenate([stored(2 * t), stored(2 * t + 1)], 0)
-            sym = jnp.where(k <= j, s, 0.0) + jnp.where(k < j, s, 0.0).T
+            sym = symmetric(inv_ref[pair + q])
             for h in range(2):
                 i = lo + h - side * per
 
@@ -657,7 +696,7 @@
         push(n).wait()
 
 
-def carry_job(at, scalars, order, terr_stored, terr_all, whitened, directions, edge, v, pres, out):
+def carry_job(at, scalars, order, terr_all, whitened, directions, edge, v, pres, out):
     own = whitened.shape[0]
     cols = directions.shape[1]
     n_row = pres[0].shape[0]
@@ -666,7 +705,7 @@
     any_spec = pl.BlockSpec(memory_space=pl.ANY)
     return pl.pallas_call(
         functools.partial(carry_kernel, at, n_row),
-        in_specs=[smem] * 2 + [vmem] * 6 + [any_spec] * 3,
+        in_specs=[smem] * 2 + [vmem] * 5 + [any_spec] * 3,
         out_specs=[vmem, any_spec],
         out_shape=[jax.ShapeDtypeStruct((own, cols), jnp.float32), out],
         scratch_shapes=[
@@ -681,7 +720,7 @@
         cost_estimate=pl.CostEstimate(
             flops=6 * own * whitened.shape[1] * cols, bytes_accessed=60000000, transcendentals=0
         ),
-    )(scalars, order, terr_stored, terr_all, whitened, directions, edge, v, *pres)
+    )(scalars, order, terr_all, whitened, directions, edge, v, *pres)
 
 
 def tile_kernel(parts, rows_at, s_ref, *refs):
@@ -879,7 +918,7 @@
 
     out = jax.ShapeDtypeStruct((n_row * own, n_col * own), jnp.float32)
     products, out = carry_job(
-        at, scalars, block_order, terr_stored, terr_all, whitened, directions, edge,
+        at, scalars, block_order, terr_all, whitened, directions, edge,
         v, pres, out,
     )
     early = lambda late, y, h: late == 1 - y

time: 241 us -> 236 us (0.979)
  Pallas kernels: 229 us -> 223 us
    pallas_call x1, Pallas kernels: 165 us -> 160 us  [exchange(): pl.pallas_call(functools.partial(exchange_kernel, n_row, n_col, parts), i...]
  transfers between devices with their start and end apart: 4 -> 4, of which waited for: 3 -> 3; matrix products, arithmetic and copies ran while one was open for 1% -> 1% of each run, Pallas kernels for 17% -> 18%
where the time goes in v3:
time: 236 us; the launch traced here: 235 us
  Pallas kernels  223 us (94%)
  starting transfers between devices  4.1 us (2%)
  local copies, waits for them, and re-layouts  3.74 us (2%)
    pallas_call x1, Pallas kernels, exchange(): pl.pallas_call(functools.partial(exchange_kernel, n_row, n_col, parts), i...  160 us
    pallas_call x2, Pallas kernels, tile_job(): pl.pallas_call(functools.partial(tile_kernel, made, rows_at), grid_spec=p...  33.8 us
    pallas_call x1, Pallas kernels, carry_job(): pl.pallas_call(functools.partial(carry_kernel, at, n_row), in_specs=[smem...  22 us
    pallas_call x1, Pallas kernels, whiten_rows(): pl.pallas_call(whiten_kernel, grid=(total // width,), in_specs=[pl.BlockS...  7.77 us
  transfers between devices with their start and end apart: 4, of which 3 were waited for; matrix products, arithmetic and copies ran while one was open for 1% of the time, Pallas kernels for 18%

profile of v3, /device:TPU:0, one launch (start us, length us, event | category | flops | bytes accessed | tf_op | source)
XLA Modules:
  0.0 235.1 jit_solution(11928190799857116624)
XLA Ops:
  0.6 7.8 %whiten.1.w_ref = bf16[576,2048]{1,0:T(8,128)(2,1)} custom-call(bf16[576,2048]{1,0:T(8,128)(2,1)} %dp_ref.1, bf16[576,2048]{1,0:T(8,128)(2,1)} %dp_ref.1, bf16[2048,2048]{1,0:T(8,128)(2,1)} %fp_ref.1, bf16[2048,2048]{1,0:T(8,128)(2,1)} %fp_ref.1, s32[1,2048]{1,0:T(1,128)} %bitcast.9, s32[1,2048]{1,0:T(1,128)} %bitcast.10), custom_call_target="tpu_custom_call" | custom-call | flops 2415919104 | bytes 9437184 | tf_op jit(solution)/shard_map/whiten/pallas_call | solution.py:119
  8.4 159.8 %exchange.1 = (bf16[4,576,2048]{2,1,0:T(8,128)(2,1)}, bf16[576,2048]{1,0:T(8,128)(2,1)}, bf16[288,2048]{1,0:T(8,128)(2,1)}, bf16[288,2048]{1,0:T(8,128)(2,1)}, b...) custom-call(bf16[576,2048]{1,0:T(8,128)(2,1)} %whiten.1.w_ref, ...), custom_call_target="tpu_custom_call" | custom-call | flops 1000000 | bytes 47185920 | tf_op jit(solution)/shard_map/exchange/pallas_call | solution.py:539
  168.2 0.1 collective-permute-start
  168.3 2.0 collective-permute-start.3
  170.3 0.0 collective-permute-start.1
  170.3 2.0 collective-permute-start.2
  172.3 0.7 dynamic-slice_bitcast_fusion.1
  173.0 0.7 dynamic-slice_bitcast_fusion
  173.7 0.7 pad_add_fusion.s_ref
  174.4 22.0 %carry.1 = (f32[576,256]{1,0:T(8,128)}, f32[2304,4608]{1,0:T(8,128)}) custom-call(s32[33]{0:T(128)} %pad_add_fusion.s_ref, s32[36]{0:T(128)} %order_ref.1, bf16[8,336,128]{2,1,0:T(8,128)(2,1)} %get-tuple-element.28.t_ref, bf16[576,2048]{1,0:T(8,128)(2,1)} %whiten.1.w_ref, f32[576,256]{1,0:T(8,128)} %d_ref.5, f32[64,256]{1,0:T(8,128)} %get-tuple-element.29.e_ref, ...), custom_call_target="tpu_custom_call" | custom-call | flops 1811939328 | bytes 60000000 | tf_op jit(solution)/shard_map/carry/pallas_call | solution.py:706
  196.4 0.9 collective-permute-done.refs_2_.refs_1_
  197.3 0.0 copy-start
  197.3 0.1 collective-permute-done.3.refs_5_.refs_6_
  197.4 0.0 copy-start.1
  197.4 0.9 copy-done
  198.3 0.4 copy-done.1
  198.8 19.8 %shard_map.95.refs_9_ = f32[2304,4608]{1,0:T(8,128)} custom-call(s32[33]{0:T(128)} %pad_add_fusion.s_ref, bf16[288,2048]{1,0:T(8,128)(2,1)} %get-tuple-element.20.refs_0_, bf16[288,2048]{1,0:T(8,128)(2,1)} %get-tuple-element.26.refs_1_, bf16[288,2048]{1,0:T(8,128)(2,1)} %copy-done, ...), custom_call_target="tpu_custom_call", output_to_operand_aliasing={{}: (12, {})} | custom-call | flops 10871635968 | bytes 20054016 | tf_op jit(solution)/shard_map/pallas_call | solution.py:825
  218.6 1.3 collective-permute-done.1.refs_3_
  219.9 0.0 copy-start.2
  219.9 0.0 collective-permute-done.2.refs_4_
  220.0 1.0 copy-done.2
  220.9 14.0 %shard_map.96 = f32[2304,4608]{1,0:T(8,128)} custom-call(s32[33]{0:T(128)} %pad_add_fusion.s_ref, bf16[576,2048]{1,0:T(8,128)(2,1)} %get-tuple-element.19.refs_8_.refs_0_, bf16[288,2048]{1,0:T(8,128)(2,1)} %copy-done, bf16[288,2048]{1,0:T(8,128)(2,1)} %get-tuple-element.21.refs_3_.refs_2_, ...), custom_call_target="tpu_custom_call", output_to_operand_aliasing={{}: (10, {})} | custom-call | flops 6039797760 | bytes 15335424 | tf_op jit(solution)/shard_map/pallas_call | solution.py:825
Async XLA Ops:
  168.2 29.1 %collective-permute-start = (bf16[288,2048]{1,0:T(8,128)(2,1)}, bf16[288,2048]{1,0:T(8,128)(2,1)S(1)}, u32[]{:S(2)}, u32[]{:S(2)}) collective-permute-start(bf16[288,2048]{1,0:T(8,128)(2,1)} %get-tuple-element.20.refs_0_), channel_id=1, source_target_pairs={{2,0},{4,2},{6,4},{7,6},{5,7},{3,5},{1,3},{0,1},{10,8},{12,10},{14... | collective-permute-start | bytes 3538952 | tf_op jit(solution)/shard_map/ppermute | solution.py:861
  168.3 29.1 %collective-permute-start.3 = (bf16[288,2048]{1,0:T(8,128)(2,1)}, bf16[288,2048]{1,0:T(8,128)(2,1)S(1)}, u32[]{:S(2)}, u32[]{:S(2)}) collective-permute-start(bf16[288,2048]{1,0:T(8,128)(2,1)} %get-tuple-element.23.refs_7_), channel_id=1, source_target_pairs={{0,2},{2,4},{4,6},{6,7},{7,5},{5,3},{3,1},{1,0},{8,10},{10,12},{12... | collective-permute-start | bytes 3538952 | tf_op jit(solution)/shard_map/ppermute | solution.py:861
  170.3 49.6 %collective-permute-start.1 = (bf16[288,2048]{1,0:T(8,128)(2,1)}, bf16[288,2048]{1,0:T(8,128)(2,1)S(1)}, u32[]{:S(2)}, u32[]{:S(2)}) collective-permute-start(bf16[288,2048]{1,0:T(8,128)(2,1)} %get-tuple-element.22.refs_4_.refs_5_), channel_id=1, source_target_pairs={{0,2},{2,4},{4,6},{6,7},{7,5},{5,3},{3,1},{1,0},{8,10},{10,12},{12... | collective-permute-start | bytes 3538952 | tf_op jit(solution)/shard_map/ppermute | solution.py:861
  170.3 49.6 %collective-permute-start.2 = (bf16[288,2048]{1,0:T(8,128)(2,1)}, bf16[288,2048]{1,0:T(8,128)(2,1)}, u32[]{:S(2)}, u32[]{:S(2)}) collective-permute-start(bf16[288,2048]{1,0:T(8,128)(2,1)} %get-tuple-element.21.refs_3_.refs_2_), channel_id=1, source_target_pairs={{2,0},{4,2},{6,4},{7,6},{5,7},{3,5},{1,3},{0,1},{10,8},{12,10},{14... | collective-permute-start | bytes 3538952 | tf_op jit(solution)/shard_map/ppermute | solution.py:861
  197.3 1.0 copy-start
  197.4 1.4 copy-start.1
  219.9 1.0 copy-start.2

commit v4 on v3

--- a/solution.py
+++ b/solution.py
@@ -11,6 +11,7 @@
 HIGH = lax.Precision.HIGHEST
 NT = (((1,), (1,)), ((), ()))
 MESH = pl.DeviceIdType.MESH
+VMEM_BYTES = 67043328
 
 
 def dot_high(a, b):
@@ -571,7 +572,7 @@
         ],
         name="exchange",
         compiler_params=pltpu.CompilerParams(
-            collective_id=0, has_side_effects=True, vmem_limit_bytes=60 * 1024 * 1024
+            collective_id=0, has_side_effects=True, vmem_limit_bytes=VMEM_BYTES
         ),
         cost_estimate=pl.CostEstimate(
             flops=1000000, bytes_accessed=40 * own * total, transcendentals=0
@@ -716,7 +717,7 @@
             pltpu.SemaphoreType.DMA((3 * n_row,)),
         ],
         name="carry",
-        compiler_params=pltpu.CompilerParams(vmem_limit_bytes=60 * 1024 * 1024),
+        compiler_params=pltpu.CompilerParams(vmem_limit_bytes=VMEM_BYTES),
         cost_estimate=pl.CostEstimate(
             flops=6 * own * whitened.shape[1] * cols, bytes_accessed=60000000, transcendentals=0
         ),
@@ -839,7 +840,7 @@
         ),
         out_shape=jax.ShapeDtypeStruct(out.shape, out.dtype),
         input_output_aliases={2 + len(arrays): 0},
-        compiler_params=pltpu.CompilerParams(vmem_limit_bytes=60 * 1024 * 1024),
+        compiler_params=pltpu.CompilerParams(vmem_limit_bytes=VMEM_BYTES),
         cost_estimate=pl.CostEstimate(
             flops=2 * count * own * columns * total,
             bytes_accessed=2 * count * own * total + 4 * count * own * columns,

time: 236 us -> 235 us (level)
  local copies, waits for them, and re-layouts: 3.74 us -> 1.38 us
where the time goes in v4:
time: 235 us; the launch traced here: 234 us
  Pallas kernels  223 us (95%)
  starting transfers between devices  4.1 us (2%)
  waiting for transfers between devices  3.88 us (2%)
    pallas_call x1, Pallas kernels, exchange(): pl.pallas_call(functools.partial(exchange_kernel, n_row, n_col, parts), i...  160 us
    pallas_call x2, Pallas kernels, tile_job(): pl.pallas_call(functools.partial(tile_kernel, made, rows_at), grid_spec=p...  33.8 us
    pallas_call x1, Pallas kernels, carry_job(): pl.pallas_call(functools.partial(carry_kernel, at, n_row), in_specs=[smem...  22 us
    pallas_call x1, Pallas kernels, whiten_rows(): pl.pallas_call(whiten_kernel, grid=(total // width,), in_specs=[pl.BlockS...  7.74 us
  transfers between devices with their start and end apart: 4, of which 3 were waited for; matrix products, arithmetic and copies ran while one was open for 1% of the time, Pallas kernels for 18%

profile of v4, /device:TPU:0, one launch (start us, length us, event | category | flops | bytes accessed | tf_op | source)
XLA Modules:
  0.0 234.2 jit_solution(8097687388195783092)
XLA Ops:
  0.6 7.7 %whiten.1.w_ref = bf16[576,2048]{1,0:T(8,128)(2,1)} custom-call(bf16[576,2048]{1,0:T(8,128)(2,1)} %dp_ref.1, bf16[576,2048]{1,0:T(8,128)(2,1)} %dp_ref.1, bf16[2048,2048]{1,0:T(8,128)(2,1)} %fp_ref.1, bf16[2048,2048]{1,0:T(8,128)(2,1)} %fp_ref.1, s32[1,2048]{1,0:T(1,128)} %bitcast.9, s32[1,2048]{1,0:T(1,128)} %bitcast.10), custom_call_target="tpu_custom_call" | custom-call | flops 2415919104 | bytes 9437184 | tf_op jit(solution)/shard_map/whiten/pallas_call | solution.py:120
  8.4 159.8 %exchange.1 = (bf16[4,576,2048]{2,1,0:T(8,128)(2,1)}, bf16[576,2048]{1,0:T(8,128)(2,1)}, bf16[288,2048]{1,0:T(8,128)(2,1)}, bf16[288,2048]{1,0:T(8,128)(2,1)}, b...) custom-call(bf16[576,2048]{1,0:T(8,128)(2,1)} %whiten.1.w_ref, ...), custom_call_target="tpu_custom_call" | custom-call | flops 1000000 | bytes 47185920 | tf_op jit(solution)/shard_map/exchange/pallas_call | solution.py:540
  168.2 0.1 collective-permute-start
  168.3 2.0 collective-permute-start.3
  170.3 0.0 collective-permute-start.1
  170.3 2.0 collective-permute-start.2
  172.3 0.7 dynamic-slice_bitcast_fusion.1
  173.0 0.7 dynamic-slice_bitcast_fusion
  173.7 0.6 pad_add_fusion.s_ref
  174.3 22.0 %carry.1 = (f32[576,256]{1,0:T(8,128)}, f32[2304,4608]{1,0:T(8,128)}) custom-call(s32[33]{0:T(128)} %pad_add_fusion.s_ref, s32[36]{0:T(128)} %order_ref.1, bf16[8,336,128]{2,1,0:T(8,128)(2,1)} %get-tuple-element.28.t_ref, bf16[576,2048]{1,0:T(8,128)(2,1)} %whiten.1.w_ref, f32[576,256]{1,0:T(8,128)} %d_ref.5, f32[64,256]{1,0:T(8,128)} %get-tuple-element.29.e_ref, ...), custom_call_target="tpu_custom_call" | custom-call | flops 1811939328 | bytes 60000000 | tf_op jit(solution)/shard_map/carry/pallas_call | solution.py:707
  196.3 1.1 collective-permute-done.refs_2_.refs_1_
  197.4 0.1 collective-permute-done.3.refs_5_.refs_6_
  197.5 19.8 %shard_map.95.refs_9_ = f32[2304,4608]{1,0:T(8,128)} custom-call(s32[33]{0:T(128)} %pad_add_fusion.s_ref, bf16[288,2048]{1,0:T(8,128)(2,1)} %get-tuple-element.20.refs_0_, bf16[288,2048]{1,0:T(8,128)(2,1)} %get-tuple-element.26.refs_1_, bf16[288,2048]{1,0:T(8,128)(2,1)} %collective-permute-done.refs_2_.refs_1_, ...), custom_call_target="tpu_custom_call", output_to_operand_aliasing={{}: (12, {})} | custom-call | flops 10871635968 | bytes 20054016 | tf_op jit(solution)/shard_map/pallas_call | solution.py:826
  217.3 2.7 %collective-permute-done.1.refs_3_ = bf16[288,2048]{1,0:T(8,128)(2,1)} collective-permute-done((bf16[288,2048]{1,0:T(8,128)(2,1)}, bf16[288,2048]{1,0:T(8,128)(2,1)}, u32[]{:S(2)}, u32[]{:S(2)}) %collective-permute-start.1) | collective-permute-done | bytes 1179680 | tf_op jit(solution)/shard_map/ppermute | solution.py:862
  220.0 0.0 collective-permute-done.2.refs_4_
  220.0 14.0 %shard_map.96 = f32[2304,4608]{1,0:T(8,128)} custom-call(s32[33]{0:T(128)} %pad_add_fusion.s_ref, bf16[576,2048]{1,0:T(8,128)(2,1)} %get-tuple-element.19.refs_8_.refs_0_, bf16[288,2048]{1,0:T(8,128)(2,1)} %collective-permute-done.refs_2_.refs_1_, bf16[288,2048]{1,0:T(8,128)(2,1)} %get-tuple-element.21.refs_3_.refs_2_, ...), custom_call_target="tpu_custom_call", output_to_operand_aliasing={{}: (10, {})} | custom-call | flops 6039797760 | bytes 15335424 | tf_op jit(solution)/shard_map/pallas_call | solution.py:826
Async XLA Ops:
  168.2 29.2 %collective-permute-start = (bf16[288,2048]{1,0:T(8,128)(2,1)}, bf16[288,2048]{1,0:T(8,128)(2,1)}, u32[]{:S(2)}, u32[]{:S(2)}) collective-permute-start(bf16[288,2048]{1,0:T(8,128)(2,1)} %get-tuple-element.20.refs_0_), channel_id=1, source_target_pairs={{2,0},{4,2},{6,4},{7,6},{5,7},{3,5},{1,3},{0,1},{10,8},{12,10},{14... | collective-permute-start | bytes 3538952 | tf_op jit(solution)/shard_map/ppermute | solution.py:862
  168.3 29.2 %collective-permute-start.3 = (bf16[288,2048]{1,0:T(8,128)(2,1)}, bf16[288,2048]{1,0:T(8,128)(2,1)}, u32[]{:S(2)}, u32[]{:S(2)}) collective-permute-start(bf16[288,2048]{1,0:T(8,128)(2,1)} %get-tuple-element.23.refs_7_), channel_id=1, source_target_pairs={{0,2},{2,4},{4,6},{6,7},{7,5},{5,3},{3,1},{1,0},{8,10},{10,12},{12... | collective-permute-start | bytes 3538952 | tf_op jit(solution)/shard_map/ppermute | solution.py:862
  170.3 49.7 %collective-permute-start.1 = (bf16[288,2048]{1,0:T(8,128)(2,1)}, bf16[288,2048]{1,0:T(8,128)(2,1)}, u32[]{:S(2)}, u32[]{:S(2)}) collective-permute-start(bf16[288,2048]{1,0:T(8,128)(2,1)} %get-tuple-element.22.refs_4_.refs_5_), channel_id=1, source_target_pairs={{0,2},{2,4},{4,6},{6,7},{7,5},{5,3},{3,1},{1,0},{8,10},{10,12},{12... | collective-permute-start | bytes 3538952 | tf_op jit(solution)/shard_map/ppermute | solution.py:862
  170.3 49.7 %collective-permute-start.2 = (bf16[288,2048]{1,0:T(8,128)(2,1)}, bf16[288,2048]{1,0:T(8,128)(2,1)}, u32[]{:S(2)}, u32[]{:S(2)}) collective-permute-start(bf16[288,2048]{1,0:T(8,128)(2,1)} %get-tuple-element.21.refs_3_.refs_2_), channel_id=1, source_target_pairs={{2,0},{4,2},{6,4},{7,6},{5,7},{3,5},{1,3},{0,1},{10,8},{12,10},{14... | collective-permute-start | bytes 3538952 | tf_op jit(solution)/shard_map/ppermute | solution.py:862

commit v5 on v4

--- a/solution.py
+++ b/solution.py
@@ -95,9 +95,11 @@
     return x[:, 2 * n :] + x[:, n : 2 * n] + x[:, :n]
 
 
-def whiten_kernel(d_ref, dp_ref, f_ref, fp_ref, ar_ref, arp_ref, w_ref):
+def whiten_kernel(d_ref, f_ref, fp_ref, ar_ref, arp_ref, w_ref):
     b = pl.program_id(0)
     width = f_ref.shape[0]
+    own = d_ref[:, pl.ds(pl.multiple_of(b * width, width), width)]
+    before = d_ref[:, pl.ds(pl.multiple_of(jnp.maximum(b - 1, 0) * width, width), width)]
     zero = jnp.zeros((width, width), jnp.float32)
     k = lax.broadcasted_iota(jnp.int32, (width, width), 0)
     j = lax.broadcasted_iota(jnp.int32, (width, width), 1)
@@ -106,9 +108,9 @@
     keep_prev = (column == arp_ref[...]) & (b > 0)
     here = jnp.where(keep, f_ref[...].astype(jnp.float32), zero).astype(jnp.bfloat16)
     prev = jnp.where(keep_prev, fp_ref[...].astype(jnp.float32), zero).astype(jnp.bfloat16)
-    mixed = lax.dot_general(d_ref[...], here, NT, preferred_element_type=jnp.float32)
-    mixed += lax.dot_general(dp_ref[...], prev, NT, preferred_element_type=jnp.float32)
-    w_ref[...] = (d_ref[...].astype(jnp.float32) + mixed).astype(jnp.bfloat16)
+    mixed = lax.dot_general(own, here, NT, preferred_element_type=jnp.float32)
+    mixed += lax.dot_general(before, prev, NT, preferred_element_type=jnp.float32)
+    w_ref[...] = (own.astype(jnp.float32) + mixed).astype(jnp.bfloat16)
 
 
 def whiten_rows(design, arc_filter, arc_of_row):
@@ -121,8 +123,7 @@
         whiten_kernel,
         grid=(total // width,),
         in_specs=[
-            pl.BlockSpec((own, width), here),
-            pl.BlockSpec((own, width), prev),
+            pl.BlockSpec((own, total), lambda b: (0, 0)),
             pl.BlockSpec((width, width), lambda b: (b, b)),
             pl.BlockSpec((width, width), lambda b: (b, jnp.maximum(b - 1, 0))),
             pl.BlockSpec((1, width), here),
@@ -134,7 +135,7 @@
         cost_estimate=pl.CostEstimate(
             flops=4 * own * total * width, bytes_accessed=8 * own * total, transcendentals=0
         ),
-    )(design, design, arc_filter, arc_filter, row, row)
+    )(design, arc_filter, arc_filter, row, row)
 
 
 def masks_of(n):

time: 235 us -> 235 us (level)
  no operation moved by 1% of the time
where the time goes in v5:
time: 235 us; the launch traced here: 234 us
  Pallas kernels  223 us (95%)
  starting transfers between devices  4.1 us (2%)
  waiting for transfers between devices  3.88 us (2%)
    pallas_call x1, Pallas kernels, exchange(): pl.pallas_call(functools.partial(exchange_kernel, n_row, n_col, parts), i...  160 us
    pallas_call x2, Pallas kernels, tile_job(): pl.pallas_call(functools.partial(tile_kernel, made, rows_at), grid_spec=p...  33.8 us
    pallas_call x1, Pallas kernels, carry_job(): pl.pallas_call(functools.partial(carry_kernel, at, n_row), in_specs=[smem...  22 us
    pallas_call x1, Pallas kernels, whiten_rows(): pl.pallas_call(whiten_kernel, grid=(total // width,), in_specs=[pl.BlockS...  7.64 us
  transfers between devices with their start and end apart: 4, of which 3 were waited for; matrix products, arithmetic and copies ran while one was open for 1% of the time, Pallas kernels for 18%

profile of v5, /device:TPU:0, one launch (start us, length us, event | category | flops | bytes accessed | tf_op | source)
XLA Modules:
  0.0 234.1 jit_solution(406494109043743635)
XLA Ops:
  0.6 7.6 %whiten.1.w_ref = bf16[576,2048]{1,0:T(8,128)(2,1)} custom-call(bf16[576,2048]{1,0:T(8,128)(2,1)} %d_ref.3, bf16[2048,2048]{1,0:T(8,128)(2,1)} %fp_ref.1, bf16[2048,2048]{1,0:T(8,128)(2,1)} %fp_ref.1, s32[1,2048]{1,0:T(1,128)} %bitcast.9, s32[1,2048]{1,0:T(1,128)} %bitcast.10), custom_call_target="tpu_custom_call" | custom-call | flops 2415919104 | bytes 9437184 | tf_op jit(solution)/shard_map/whiten/pallas_call | solution.py:122
  8.3 159.8 %exchange.1 = (bf16[4,576,2048]{2,1,0:T(8,128)(2,1)}, bf16[576,2048]{1,0:T(8,128)(2,1)}, bf16[288,2048]{1,0:T(8,128)(2,1)}, bf16[288,2048]{1,0:T(8,128)(2,1)}, b...) custom-call(bf16[576,2048]{1,0:T(8,128)(2,1)} %whiten.1.w_ref, ...), custom_call_target="tpu_custom_call" | custom-call | flops 1000000 | bytes 47185920 | tf_op jit(solution)/shard_map/exchange/pallas_call | solution.py:541
  168.1 0.1 collective-permute-start
  168.1 2.0 collective-permute-start.3
  170.2 0.0 collective-permute-start.1
  170.2 2.0 collective-permute-start.2
  172.2 0.7 dynamic-slice_bitcast_fusion.1
  172.9 0.7 dynamic-slice_bitcast_fusion
  173.6 0.6 pad_add_fusion.s_ref
  174.2 22.0 %carry.1 = (f32[576,256]{1,0:T(8,128)}, f32[2304,4608]{1,0:T(8,128)}) custom-call(s32[33]{0:T(128)} %pad_add_fusion.s_ref, s32[36]{0:T(128)} %order_ref.1, bf16[8,336,128]{2,1,0:T(8,128)(2,1)} %get-tuple-element.28.t_ref, bf16[576,2048]{1,0:T(8,128)(2,1)} %whiten.1.w_ref, f32[576,256]{1,0:T(8,128)} %d_ref.5, f32[64,256]{1,0:T(8,128)} %get-tuple-element.29.e_ref, ...), custom_call_target="tpu_custom_call" | custom-call | flops 1811939328 | bytes 60000000 | tf_op jit(solution)/shard_map/carry/pallas_call | solution.py:708
  196.2 1.1 collective-permute-done.refs_2_.refs_1_
  197.3 0.1 collective-permute-done.3.refs_5_.refs_6_
  197.4 19.8 %shard_map.95.refs_9_ = f32[2304,4608]{1,0:T(8,128)} custom-call(s32[33]{0:T(128)} %pad_add_fusion.s_ref, bf16[288,2048]{1,0:T(8,128)(2,1)} %get-tuple-element.20.refs_0_, bf16[288,2048]{1,0:T(8,128)(2,1)} %get-tuple-element.26.refs_1_, bf16[288,2048]{1,0:T(8,128)(2,1)} %collective-permute-done.refs_2_.refs_1_, ...), custom_call_target="tpu_custom_call", output_to_operand_aliasing={{}: (12, {})} | custom-call | flops 10871635968 | bytes 20054016 | tf_op jit(solution)/shard_map/pallas_call | solution.py:827
  217.2 2.7 %collective-permute-done.1.refs_3_ = bf16[288,2048]{1,0:T(8,128)(2,1)} collective-permute-done((bf16[288,2048]{1,0:T(8,128)(2,1)}, bf16[288,2048]{1,0:T(8,128)(2,1)}, u32[]{:S(2)}, u32[]{:S(2)}) %collective-permute-start.1) | collective-permute-done | bytes 1179680 | tf_op jit(solution)/shard_map/ppermute | solution.py:863
  219.9 0.0 collective-permute-done.2.refs_4_
  219.9 14.0 %shard_map.96 = f32[2304,4608]{1,0:T(8,128)} custom-call(s32[33]{0:T(128)} %pad_add_fusion.s_ref, bf16[576,2048]{1,0:T(8,128)(2,1)} %get-tuple-element.19.refs_8_.refs_0_, bf16[288,2048]{1,0:T(8,128)(2,1)} %collective-permute-done.refs_2_.refs_1_, bf16[288,2048]{1,0:T(8,128)(2,1)} %get-tuple-element.21.refs_3_.refs_2_, ...), custom_call_target="tpu_custom_call", output_to_operand_aliasing={{}: (10, {})} | custom-call | flops 6039797760 | bytes 15335424 | tf_op jit(solution)/shard_map/pallas_call | solution.py:827
Async XLA Ops:
  168.1 29.2 %collective-permute-start = (bf16[288,2048]{1,0:T(8,128)(2,1)}, bf16[288,2048]{1,0:T(8,128)(2,1)}, u32[]{:S(2)}, u32[]{:S(2)}) collective-permute-start(bf16[288,2048]{1,0:T(8,128)(2,1)} %get-tuple-element.20.refs_0_), channel_id=1, source_target_pairs={{2,0},{4,2},{6,4},{7,6},{5,7},{3,5},{1,3},{0,1},{10,8},{12,10},{14... | collective-permute-start | bytes 3538952 | tf_op jit(solution)/shard_map/ppermute | solution.py:863
  168.1 29.2 %collective-permute-start.3 = (bf16[288,2048]{1,0:T(8,128)(2,1)}, bf16[288,2048]{1,0:T(8,128)(2,1)}, u32[]{:S(2)}, u32[]{:S(2)}) collective-permute-start(bf16[288,2048]{1,0:T(8,128)(2,1)} %get-tuple-element.23.refs_7_), channel_id=1, source_target_pairs={{0,2},{2,4},{4,6},{6,7},{7,5},{5,3},{3,1},{1,0},{8,10},{10,12},{12... | collective-permute-start | bytes 3538952 | tf_op jit(solution)/shard_map/ppermute | solution.py:863
  170.2 49.7 %collective-permute-start.1 = (bf16[288,2048]{1,0:T(8,128)(2,1)}, bf16[288,2048]{1,0:T(8,128)(2,1)}, u32[]{:S(2)}, u32[]{:S(2)}) collective-permute-start(bf16[288,2048]{1,0:T(8,128)(2,1)} %get-tuple-element.22.refs_4_.refs_5_), channel_id=1, source_target_pairs={{0,2},{2,4},{4,6},{6,7},{7,5},{5,3},{3,1},{1,0},{8,10},{10,12},{12... | collective-permute-start | bytes 3538952 | tf_op jit(solution)/shard_map/ppermute | solution.py:863
  170.2 49.7 %collective-permute-start.2 = (bf16[288,2048]{1,0:T(8,128)(2,1)}, bf16[288,2048]{1,0:T(8,128)(2,1)}, u32[]{:S(2)}, u32[]{:S(2)}) collective-permute-start(bf16[288,2048]{1,0:T(8,128)(2,1)} %get-tuple-element.21.refs_3_.refs_2_), channel_id=1, source_target_pairs={{2,0},{4,2},{6,4},{7,6},{5,7},{3,5},{1,3},{0,1},{10,8},{12,10},{14... | collective-permute-start | bytes 3538952 | tf_op jit(solution)/shard_map/ppermute | solution.py:863
